TPU v7x, 32 devices: a whole 2x2x4 slice. The times are simulated.
32 devices in a mesh: wide: 8 (over y, x, core), narrow: 4 (over z).
Axes of the slice: x: 2, y: 2, z: 4, core: 2. Of those that a mesh axis runs over, the one named last changes fastest.
Arguments:
- tokens: float32 [4488, 768], P('wide'), may hold values from -6 to 6
- region: int32 [4488], P('wide'), may hold values from 0 to 59, as said below
- order_rank: int32 [4488], P('wide'), may hold values from 0 to 559, as said below
- box_coords: int32 [2, 4488], P(None, 'wide'), may hold values from 0 to 127
- w_query: float32 [768, 768], P(None, 'narrow'), may hold values from -0.21875 to 0.21875
- b_query: float32 [768], P('narrow'), may hold values from -3 to 3
- w_key: float32 [768, 768], P(None, 'narrow'), may hold values from -0.21875 to 0.21875
- w_value: float32 [768, 768], P(None, 'narrow'), may hold values from -0.21875 to 0.21875
- b_value: float32 [768], P('narrow'), may hold values from -0.18 to 0.18
- w_out: float32 [768, 768], P('narrow'), may hold values from -2 to 2
- b_out: float32 [768], replicated, may hold values from -2 to 2
- ln1_gain: float32 [768], replicated, may hold values from 0.1 to 1.9
- ln1_bias: float32 [768], replicated, may hold values from -2 to 2
- w_in: float32 [768, 3072], P(None, 'narrow'), may hold values from -0.21875 to 0.21875
- b_in: float32 [3072], P('narrow'), may hold values from -2 to 2
- w_down: float32 [3072, 768], P('narrow'), may hold values from -0.109375 to 0.109375
- b_down: float32 [768], replicated, may hold values from -2 to 2
- ln2_gain: float32 [768], replicated, may hold values from 0.1 to 1.9
- ln2_bias: float32 [768], replicated, may hold values from -2 to 2
- rel_order: float32 [12, 32], P('narrow'), may hold values from -3 to 3
- rel_x: float32 [12, 64], P('narrow'), may hold values from -3 to 3
- rel_y: float32 [12, 64], P('narrow'), may hold values from -3 to 3
- cotangent: float32 [4488, 768], P('wide'), may hold values from -6 to 6
Outputs:
- output: float32 [4488, 768], P('wide')
- grad_input: float32 [4488, 768], P('wide')
- grad_w_query: float32 [768, 768], P(None, 'narrow')
- grad_b_query: float32 [768], P('narrow')
- grad_w_key: float32 [768, 768], P(None, 'narrow')
- grad_w_value: float32 [768, 768], P(None, 'narrow')
- grad_b_value: float32 [768], P('narrow')
- grad_w_out: float32 [768, 768], P('narrow')
- grad_b_out: float32 [768], replicated
- grad_ln1_gain: float32 [768], replicated
- grad_ln1_bias: float32 [768], replicated
- grad_w_in: float32 [768, 3072], P(None, 'narrow')
- grad_b_in: float32 [3072], P('narrow')
- grad_w_down: float32 [3072, 768], P('narrow')
- grad_b_down: float32 [768], replicated
- grad_ln2_gain: float32 [768], replicated
- grad_ln2_bias: float32 [768], replicated
- grad_rel_order: float32 [12, 32], P('narrow')
- grad_rel_x: float32 [12, 64], P('narrow')
- grad_rel_y: float32 [12, 64], P('narrow')
Inputs may be any that keep to these rules, and one draw needn't show every extreme that they name: Each page's region ids take every value from 0 to its region count minus 1; region counts run from 2 to min(60, 561), and one page has the most. `order_rank`: within each region of a page the ranks are 0, 1, and so on up to its size minus 1, each once; no region holds more than 560 tokens, and one page has a region of exactly 560 tokens.
All inputs are finite; a program needn't handle non-finite values.
Results may differ from a plain program's by a relative error of at most 0.015.
The roundings to bfloat16 on the way count: a program that leaves them out, or rounds other values in their place, can miss the bound.
Values sent between devices are 32-bit elements; how exact they have to be, the bound alone decides.
A program may use at most 128 MiB of HBM per device.

v0:
```python
import math

import jax
import jax.numpy as jnp
from jax import lax
from jax.sharding import PartitionSpec as P

HEAD_DIM = 64
BINS1 = 32
BINS2 = 64
MAX_ORDER = 128
MAX_LAYOUT = 256
PAGE = 561


HIGHEST = lax.Precision.HIGHEST
EPSILON = 1e-05
SCORE_SCALE = 0.125


def bucket_steps(bins, reach):
    halfway = bins // 2
    exact = halfway // 2
    steps = []
    for level in range(1, halfway):
        if level < exact:
            steps.append(level)
        else:
            found = reach + 1
            for count in range(exact, reach + 2):
                value = exact + int(
                    math.log(count / exact) / math.log(reach / exact) * (halfway - exact)
                )
                if min(value, halfway - 1) >= level:
                    found = count
                    break
            steps.append(found)
    return steps


def bucket_of(offset_grid, bins, reach):
    halfway = bins // 2
    magnitude = jnp.abs(offset_grid)
    result = jnp.where(offset_grid > 0, halfway, 0).astype(jnp.int32)
    for level_start in bucket_steps(bins, reach):
        result = result + (magnitude >= level_start).astype(jnp.int32)
    return result


def norm_layer(values, gain_row, shift_row):
    average = jnp.mean(values, axis=-1, keepdims=True)
    centred = values - average
    second = jnp.mean(centred * centred, axis=-1, keepdims=True)
    return centred * lax.rsqrt(second + EPSILON) * gain_row + shift_row


def gelu_exact(values):
    return jax.nn.gelu(values, approximate=False)


def reading_place(region, order_rank):
    earlier = (region[:, None, :] < region[:, :, None]).astype(jnp.int32)
    return (jnp.sum(earlier, axis=2) + order_rank).astype(jnp.int32)


def page_buckets(place_row, across_row, down_row):
    order_bin = bucket_of(place_row[None, :] - place_row[:, None], BINS1, MAX_ORDER)
    across_bin = bucket_of(across_row[None, :] - across_row[:, None], BINS2, MAX_LAYOUT)
    down_bin = bucket_of(down_row[None, :] - down_row[:, None], BINS2, MAX_LAYOUT)
    return (order_bin, across_bin, down_bin)


def one_hot_of(grid, bins, dtype):
    return (grid[:, :, None] == jnp.arange(bins, dtype=jnp.int32)[None, None, :]).astype(dtype)


def relative_bias(tables, read_place, across, downward):

    def relative_one_page(inputs):
        grids = page_buckets(inputs[0], inputs[1], inputs[2])
        total = None
        for table, grid in zip(tables, grids):
            chooser = one_hot_of(grid, table.shape[1], jnp.float32)
            term = jnp.einsum(
                "hb,qkb->hqk", table, chooser, precision=HIGHEST, preferred_element_type=jnp.float32
            )
            total = term if total is None else total + term
        return total

    return lax.map(relative_one_page, (read_place, across, downward))


def table_grads(grad_scores, bins_list, read_place, across, downward):

    def table_one_page(inputs):
        grad_page = inputs[0]
        grids = page_buckets(inputs[1], inputs[2], inputs[3])
        return tuple(
            (
                jnp.einsum(
                    "hqk,qkb->hb",
                    grad_page,
                    one_hot_of(grid, bins, jnp.bfloat16),
                    preferred_element_type=jnp.float32,
                )
                for grid, bins in zip(grids, bins_list)
            )
        )

    per_page = lax.map(table_one_page, (grad_scores, read_place, across, downward))
    return tuple((jnp.sum(member, axis=0) for member in per_page))


def forward(tokens, lowered, biases, rel_bias):
    query_weight, key_weight, value_weight, out_weight, in_weight, down_weight = lowered
    b_query, b_value, b_out, ln1_gain, ln1_bias, b_in, b_down, ln2_gain, ln2_bias = biases
    page_count, head_count, length = (rel_bias.shape[0], rel_bias.shape[1], rel_bias.shape[2])
    shape_heads = (page_count, length, head_count, HEAD_DIM)
    tokens_low = tokens.astype(jnp.bfloat16)
    query_rows = (
        jnp.dot(tokens_low, query_weight, preferred_element_type=jnp.float32) + b_query
    ).astype(jnp.bfloat16)
    key_rows = jnp.dot(tokens_low, key_weight, preferred_element_type=jnp.float32).astype(
        jnp.bfloat16
    )
    value_rows = (
        jnp.dot(tokens_low, value_weight, preferred_element_type=jnp.float32) + b_value
    ).astype(jnp.bfloat16)
    scores = (
        jnp.einsum(
            "pqhe,pkhe->phqk",
            query_rows.reshape(shape_heads),
            key_rows.reshape(shape_heads),
            preferred_element_type=jnp.float32,
        )
        * SCORE_SCALE
        + rel_bias
    )
    row_top = jnp.max(scores, axis=-1, keepdims=True)
    raised = jnp.exp(scores - row_top)
    row_total = jnp.sum(raised, axis=-1, keepdims=True)
    attention = raised / row_total
    log_total = row_top + jnp.log(row_total)
    mixed = jnp.einsum(
        "phqk,pkhe->pqhe",
        attention.astype(jnp.bfloat16),
        value_rows.reshape(shape_heads),
        preferred_element_type=jnp.float32,
    )
    attended = mixed.reshape(tokens.shape[0], -1).astype(jnp.bfloat16)
    partial_value = jnp.dot(attended, out_weight, preferred_element_type=jnp.float32)
    branch = lax.psum(partial_value, "narrow") + b_out
    residual_one = tokens + branch
    hidden = norm_layer(residual_one, ln1_gain, ln1_bias)
    hidden_low = hidden.astype(jnp.bfloat16)
    pre_gelu = jnp.dot(hidden_low, in_weight, preferred_element_type=jnp.float32) + b_in
    active = gelu_exact(pre_gelu).astype(jnp.bfloat16)
    ff_part = jnp.dot(active, down_weight, preferred_element_type=jnp.float32)
    residual_two = hidden + (lax.psum(ff_part, "narrow") + b_down)
    output = norm_layer(residual_two, ln2_gain, ln2_bias)
    kept_values = (
        tokens_low,
        query_rows,
        key_rows,
        value_rows,
        log_total,
        attended,
        residual_one,
        hidden_low,
        pre_gelu,
        active,
        residual_two,
    )
    return (output, kept_values)


def local(
    tokens,
    region,
    order_rank,
    box_coords,
    w_query,
    b_query,
    w_key,
    w_value,
    b_value,
    w_out,
    b_out,
    ln1_gain,
    ln1_bias,
    w_in,
    b_in,
    w_down,
    b_down,
    ln2_gain,
    ln2_bias,
    rel_order,
    rel_x,
    rel_y,
    cotangent,
):
    length = PAGE
    page_count = tokens.shape[0] // length
    read_place = reading_place(
        region.reshape(page_count, length), order_rank.reshape(page_count, length)
    )
    corners = box_coords.reshape(2, page_count, length)
    rel_bias = relative_bias((rel_order, rel_x, rel_y), read_place, corners[0], corners[1])
    lowered = tuple(
        (weight.astype(jnp.bfloat16) for weight in (w_query, w_key, w_value, w_out, w_in, w_down))
    )
    query_weight, key_weight, value_weight, out_weight, in_weight, down_weight = lowered
    biases = (b_query, b_value, b_out, ln1_gain, ln1_bias, b_in, b_down, ln2_gain, ln2_bias)
    output, kept_values = forward(tokens, lowered, biases, rel_bias)
    tokens_again = lax.optimization_barrier((tokens, output))[0]
    kept_values = forward(tokens_again, lowered, biases, rel_bias)[1]
    (
        tokens_low,
        query_rows,
        key_rows,
        value_rows,
        log_total,
        attended,
        residual_one,
        hidden_low,
        pre_gelu,
        active,
        residual_two,
    ) = kept_values
    head_count = rel_bias.shape[1]
    shape_heads = (page_count, length, head_count, HEAD_DIM)
    head_width = head_count * HEAD_DIM
    _, second_back = jax.vjp(norm_layer, residual_two, ln2_gain, ln2_bias)
    grad_residual_two, grad_ln2_gain, grad_ln2_bias = second_back(cotangent)
    grad_ff = grad_residual_two.astype(jnp.bfloat16)
    grad_b_down = jnp.sum(grad_ff, axis=0, dtype=jnp.float32)
    grad_w_down = jnp.einsum("tf,td->fd", active, grad_ff, preferred_element_type=jnp.float32)
    grad_active = jnp.einsum("td,fd->tf", grad_ff, down_weight, preferred_element_type=jnp.float32)
    _, gelu_back = jax.vjp(gelu_exact, pre_gelu)
    grad_pre = gelu_back(grad_active)[0].astype(jnp.bfloat16)
    grad_b_in = jnp.sum(grad_pre, axis=0, dtype=jnp.float32)
    grad_w_in = jnp.einsum("td,tf->df", hidden_low, grad_pre, preferred_element_type=jnp.float32)
    hidden_part = jnp.einsum("tf,df->td", grad_pre, in_weight, preferred_element_type=jnp.float32)
    grad_hidden = grad_residual_two + lax.psum(hidden_part, "narrow")
    _, first_back = jax.vjp(norm_layer, residual_one, ln1_gain, ln1_bias)
    grad_residual_one, grad_ln1_gain, grad_ln1_bias = first_back(grad_hidden)
    grad_branch = grad_residual_one.astype(jnp.bfloat16)
    grad_b_out = jnp.sum(grad_branch, axis=0, dtype=jnp.float32)
    grad_w_out = jnp.einsum("tc,td->cd", attended, grad_branch, preferred_element_type=jnp.float32)
    grad_attended = jnp.einsum(
        "td,cd->tc", grad_branch, out_weight, preferred_element_type=jnp.float32
    ).astype(jnp.bfloat16)
    query_heads = query_rows.reshape(shape_heads)
    key_heads = key_rows.reshape(shape_heads)
    value_heads = value_rows.reshape(shape_heads)
    grad_heads = grad_attended.reshape(shape_heads)
    scores = (
        jnp.einsum("pqhe,pkhe->phqk", query_heads, key_heads, preferred_element_type=jnp.float32)
        * SCORE_SCALE
        + rel_bias
    )
    attention = jnp.exp(scores - log_total)
    grad_attention = jnp.einsum(
        "pqhe,pkhe->phqk", grad_heads, value_heads, preferred_element_type=jnp.float32
    )
    inner_sum = jnp.sum(attention * grad_attention, axis=-1, keepdims=True)
    grad_scores = (attention * (grad_attention - inner_sum)).astype(jnp.bfloat16)
    grad_rel_order, grad_rel_x, grad_rel_y = table_grads(
        grad_scores, (BINS1, BINS2, BINS2), read_place, corners[0], corners[1]
    )
    grad_query = (
        (
            jnp.einsum(
                "phqk,pkhe->pqhe", grad_scores, key_heads, preferred_element_type=jnp.float32
            )
            * SCORE_SCALE
        )
        .astype(jnp.bfloat16)
        .reshape(-1, head_width)
    )
    grad_key = (
        (
            jnp.einsum(
                "phqk,pqhe->pkhe", grad_scores, query_heads, preferred_element_type=jnp.float32
            )
            * SCORE_SCALE
        )
        .astype(jnp.bfloat16)
        .reshape(-1, head_width)
    )
    grad_value = (
        jnp.einsum(
            "phqk,pqhe->pkhe",
            attention.astype(jnp.bfloat16),
            grad_heads,
            preferred_element_type=jnp.float32,
        )
        .astype(jnp.bfloat16)
        .reshape(-1, head_width)
    )
    grad_b_query = jnp.sum(grad_query, axis=0, dtype=jnp.float32)
    grad_b_value = jnp.sum(grad_value, axis=0, dtype=jnp.float32)
    grad_w_query = jnp.einsum(
        "td,tc->dc", tokens_low, grad_query, preferred_element_type=jnp.float32
    )
    grad_w_key = jnp.einsum("td,tc->dc", tokens_low, grad_key, preferred_element_type=jnp.float32)
    grad_w_value = jnp.einsum(
        "td,tc->dc", tokens_low, grad_value, preferred_element_type=jnp.float32
    )
    input_part = jnp.einsum(
        "tc,dc->td", grad_query, query_weight, preferred_element_type=jnp.float32
    )
    input_part = input_part + jnp.einsum(
        "tc,dc->td", grad_key, key_weight, preferred_element_type=jnp.float32
    )
    input_part = input_part + jnp.einsum(
        "tc,dc->td", grad_value, value_weight, preferred_element_type=jnp.float32
    )
    grad_input = grad_residual_one + lax.psum(input_part, "narrow")
    (
        grad_w_query,
        grad_b_query,
        grad_w_key,
        grad_w_value,
        grad_b_value,
        grad_w_out,
        grad_b_out,
        grad_ln1_gain,
        grad_ln1_bias,
        grad_rel_order,
        grad_rel_x,
        grad_rel_y,
        grad_w_in,
        grad_b_in,
        grad_w_down,
        grad_b_down,
        grad_ln2_gain,
        grad_ln2_bias,
    ) = lax.psum(
        (
            grad_w_query,
            grad_b_query,
            grad_w_key,
            grad_w_value,
            grad_b_value,
            grad_w_out,
            grad_b_out,
            grad_ln1_gain,
            grad_ln1_bias,
            grad_rel_order,
            grad_rel_x,
            grad_rel_y,
            grad_w_in,
            grad_b_in,
            grad_w_down,
            grad_b_down,
            grad_ln2_gain,
            grad_ln2_bias,
        ),
        "wide",
    )
    return (
        output,
        grad_input,
        grad_w_query,
        grad_b_query,
        grad_w_key,
        grad_w_value,
        grad_b_value,
        grad_w_out,
        grad_b_out,
        grad_ln1_gain,
        grad_ln1_bias,
        grad_w_in,
        grad_b_in,
        grad_w_down,
        grad_b_down,
        grad_ln2_gain,
        grad_ln2_bias,
        grad_rel_order,
        grad_rel_x,
        grad_rel_y,
    )


def solution(mesh):
    in_specs = (
        P("wide", None),
        P("wide"),
        P("wide"),
        P(None, "wide"),
        P(None, "narrow"),
        P("narrow"),
        P(None, "narrow"),
        P(None, "narrow"),
        P("narrow"),
        P("narrow", None),
        P(),
        P(),
        P(),
        P(None, "narrow"),
        P("narrow"),
        P("narrow", None),
        P(),
        P(),
        P(),
        P("narrow", None),
        P("narrow", None),
        P("narrow", None),
        P("wide", None),
    )
    out_specs = (
        P("wide", None),
        P("wide", None),
        P(None, "narrow"),
        P("narrow"),
        P(None, "narrow"),
        P(None, "narrow"),
        P("narrow"),
        P("narrow", None),
        P(),
        P(),
        P(),
        P(None, "narrow"),
        P("narrow"),
        P("narrow", None),
        P(),
        P(),
        P(),
        P("narrow", None),
        P("narrow", None),
        P("narrow", None),
    )
    return jax.shard_map(local, mesh=mesh, in_specs=in_specs, out_specs=out_specs, check_vma=False)
```

profile of v0, /device:TPU:0, one launch (start us, length us, event | category | flops | bytes accessed | tf_op | source)
XLA Modules:
  0.0 774.5 jit_solution(14613207930424786507)
XLA Ops:
  8.0 13.1 %fusion.116 = s32[561]{0:T(1024)S(1)} fusion(s32[561]{0:T(1024)} %param.24), kind=kLoop, calls=%fused_computation.185 | loop fusion | flops 943602 | bytes 4488 | tf_op jit(solution)/shard_map/reduce_sum | solution.py:63
  21.8 2.5 convert_add_fusion.2
  24.3 9.5 %convert_add_fusion = (s32[561,561]{0,1:T(8,128)S(1)}, s32[561,561]{0,1:T(8,128)S(1)}) fusion(s32[561]{0:T(1024)S(1)} %get-tuple-element.77, s32[561]{0:T(1024)S(1)} %get-tuple-element.76), kind=kLoop, calls=%fused_computation.182 | loop fusion | flops 61055736 | bytes 2522256 | tf_op jit(solution)/shard_map/while/body/eval_jaxpr/add | solution.py:46
  33.8 28.1 %fusion.2 = f32[561,561,3]{0,2,1:T(4,128)S(1)} fusion(s32[561,561]{0,1:T(8,128)S(1)} %get-tuple-element.126, f32[3,64]{1,0:T(4,128)S(1)} %copy-done), kind=kOutput, calls=%fused_computation.3 | convolution fusion | flops 745259328 | bytes 5036304 | tf_op jit(solution)/shard_map/while/body/eval_jaxpr/hb,qkb->hqk/dot_general | solution.py:84
  61.9 29.6 %fusion.4 = f32[561,561,3]{0,2,1:T(4,128)} fusion(s32[561,561]{0,1:T(8,128)S(1)} %get-tuple-element.127, f32[3,64]{1,0:T(4,128)S(1)} %copy-done.60), kind=kOutput, calls=%fused_computation.6 | convolution fusion | flops 745259328 | bytes 5036304 | tf_op jit(solution)/shard_map/while/body/eval_jaxpr/hb,qkb->hqk/dot_general | solution.py:84
  91.5 15.8 %fusion.10 = f32[561,561,3]{0,2,1:T(4,128)} fusion(s32[561,561]{0,1:T(8,128)S(1)} %convert_add_fusion.2, f32[3,32]{1,0:T(4,128)S(1)} %copy-done.61), kind=kOutput, calls=%fused_computation.13 | convolution fusion | flops 372629664 | bytes 5035920 | tf_op jit(solution)/shard_map/while/body/eval_jaxpr/hb,qkb->hqk/dot_general | solution.py:84
  108.9 5.0 copy_add_fusion
  118.7 4.9 fusion.120
  125.5 77.9 %all-reduce.10.cloned.1.call-done = f32[561,768]{1,0:T(8,128)} async-done(((f32[561,768]{1,0:T(8,128)}), f32[561,768]{1,0:T(8,128)}) %all-reduce.10.cloned.1.call-update) | async-done | bytes 1723408 | tf_op jit(solution)/shard_map/psum | solution.py:152
  205.9 8.9 %fusion.119 = f32[561,768]{1,0:T(8,128)} fusion(f32[561,768]{1,0:T(8,128)S(1)} %get-tuple-element.114, f32[768]{0:T(1024)S(1)} %copy-done.59, f32[768]{0:T(1024)S(1)} %copy-done.52, f32[768]{0:T(1024)S(1)} %copy-done.48, f32[561]{0:T(1024)S(1)} %add_rsqrt_fusion.1, f32[561]{0:T(1024)S(1)} %broadcast_multiply_fusion.3, f32[768,768]{1,0:T(8,128)} %param.38, ...), kind=kOutput, calls=%fused_computation.194 | convolution fusion | flops 1355334912 | bytes 8179080 | tf_op jit(solution)/shard_map/dot_general | solution.py:158
  214.9 74.4 %all-reduce.12.cloned.1.call-done = f32[561,768]{1,0:T(8,128)} async-done(((f32[561,768]{1,0:T(8,128)}), f32[561,768]{1,0:T(8,128)}) %all-reduce.12.cloned.1.call-update) | async-done | bytes 1723408 | tf_op jit(solution)/shard_map/psum | solution.py:159
  289.3 2.1 fusion.256
  303.8 74.0 %all-reduce.14.cloned.1.call-done = f32[561,768]{1,0:T(8,128)} async-done(((f32[561,768]{1,0:T(8,128)}), f32[561,768]{1,0:T(8,128)}) %all-reduce.14.cloned.1.call-update) | async-done | bytes 1723408 | tf_op jit(solution)/shard_map/psum | solution.py:152
  380.1 6.0 multiply_convert_fusion.1
  387.1 2.1 fusion.189
  389.2 74.4 %all-reduce.16.cloned.1.call-done = f32[561,768]{1,0:T(8,128)} async-done(((f32[561,768]{1,0:T(8,128)}), f32[561,768]{1,0:T(8,128)}) %all-reduce.16.cloned.1.call-update) | async-done | bytes 1723408 | tf_op jit(solution)/shard_map/psum | solution.py:159
  463.6 2.1 fusion.253
  471.7 2.0 convert_reduce_fusion.1
  474.6 2.1 fusion.223
  476.8 74.3 %all-reduce.18.cloned.1.call-done = f32[561,768]{1,0:T(8,128)} async-done(((f32[561,768]{1,0:T(8,128)}), f32[561,768]{1,0:T(8,128)}) %all-reduce.18.cloned.1.call-update) | async-done | bytes 1723408 | tf_op jit(solution)/shard_map/psum | solution.py:244
  551.2 2.6 multiply_reduce_fusion.2
  565.4 4.0 fusion.264
  569.4 2.9 fusion.248
  572.5 2.3 fusion.263
  580.0 8.8 %fusion.131 = f32[3,32]{1,0:T(4,128)S(1)} fusion(s32[561,561]{0,1:T(8,128)} %copy-done.34, bf16[3,561,561]{1,2,0:T(8,128)(2,1)S(1)} %copy-done.8), kind=kOutput, calls=%fused_computation.207 | convolution fusion | flops 70497504 | bytes 3147594 | tf_op jit(solution)/shard_map/while/body/eval_jaxpr/hqk,qkb->hb/dot_general | solution.py:100
  588.9 14.6 %fusion.134 = f32[3,64]{1,0:T(4,128)S(1)} fusion(s32[561,561]{0,1:T(8,128)S(1)} %copy-done.38, bf16[3,561,561]{1,2,0:T(8,128)(2,1)S(1)} %copy-done.8), kind=kOutput, calls=%fused_computation.208 | convolution fusion | flops 140995008 | bytes 3147978 | tf_op jit(solution)/shard_map/while/body/eval_jaxpr/hqk,qkb->hb/dot_general | solution.py:100
  603.5 14.9 %fusion.137 = f32[3,64]{1,0:T(4,128)S(1)} fusion(s32[561,561]{0,1:T(8,128)S(1)} %copy-done.36, bf16[3,561,561]{1,2,0:T(8,128)(2,1)S(1)} %copy-done.8), kind=kOutput, calls=%fused_computation.209 | convolution fusion | flops 140995008 | bytes 3147978 | tf_op jit(solution)/shard_map/while/body/eval_jaxpr/hqk,qkb->hb/dot_general | solution.py:100
  618.4 25.3 %all-reduce = (f32[192]{0:T(256)}, f32[192]{0:T(256)}, f32[768]{0:T(1024)}, f32[768]{0:T(1024)}, f32[768]{0:T(1024)}, /*index=5*/f32[768]{0:T(1024)}, f32[768]{0...) all-reduce(f32[192]{0:T(256)S(1)} %reduce_sum.254, ...), channel_id=1, replica_groups=mesh['wide'=8,'narrow'=4] {'wide'}, use_global_device_ids=true, to_apply=%region_26.27 | all-reduce | flops 6240 | bytes 49920 | tf_op jit(solution)/shard_map/psum | solution.py:339
  643.7 3.4 add_add_fusion.7
  647.1 110.7 %all-reduce.22.cloned.1.call-done = (f32[768,192]{0,1:T(8,128)}, f32[768,192]{0,1:T(8,128)}, f32[768,192]{0,1:T(8,128)}, f32[192,768]{1,0:T(8,128)}, f32[768,768]{1,0:T(8,128)}, /*index=5*/f32[768,768]{1,0:T(8,128)}) async-done(((f32[768,192]{0,1:T(8,128)}, f32[768,192]{0,1:T(8,128)}, f32[768,192]{0,1:T(8,128)}, f32[192,768]{1,0:T(8,128)}, f32[768,768]{1,0:T(8,128)}, /*index=5*/f32[768,768]{1,0:T(8,128)}), ...) | async-done | bytes 7077904 | tf_op jit(solution)/shard_map/psum | solution.py:339
  757.8 2.0 copy.114
  759.8 2.1 copy.115
  (212 shorter events, 57.2 us)
Async XLA Ops:
  7.2 26.6 %copy-start = (f32[3,64]{1,0:T(4,128)S(1)}, f32[3,64]{1,0:T(4,128)}, u32[]{:S(2)}) copy-start(f32[3,64]{1,0:T(4,128)} %param.44) | copy-start | bytes 2308
  7.2 196.2 %all-reduce.10.cloned.1.call-start = ((), (), s32[]{:S(2)}) async-start(), calls=%async_computation | async-start | bytes 3489792 | tf_op jit(solution)/shard_map/psum | solution.py:152
  24.3 67.3 %copy-start.34 = (s32[561,561]{0,1:T(8,128)}, s32[561,561]{0,1:T(8,128)S(1)}, u32[]{:S(2)}) copy-start(s32[561,561]{0,1:T(8,128)S(1)} %convert_add_fusion.2) | copy-start | bytes 3776656
  33.8 28.1 %copy-start.35 = (s32[561,561]{0,1:T(8,128)}, s32[561,561]{0,1:T(8,128)S(1)}, u32[]{:S(2)}) copy-start(s32[561,561]{0,1:T(8,128)S(1)} %get-tuple-element.126) | copy-start | bytes 3776656
  33.8 28.1 %copy-start.37 = (s32[561,561]{0,1:T(8,128)}, s32[561,561]{0,1:T(8,128)S(1)}, u32[]{:S(2)}) copy-start(s32[561,561]{0,1:T(8,128)S(1)} %get-tuple-element.127) | copy-start | bytes 3776656
  33.8 28.1 %copy-start.60 = (f32[3,64]{1,0:T(4,128)S(1)}, f32[3,64]{1,0:T(4,128)}, u32[]{:S(2)}) copy-start(f32[3,64]{1,0:T(4,128)} %param.43) | copy-start | bytes 2308
  61.9 29.6 %copy-start.61 = (f32[3,32]{1,0:T(4,128)S(1)}, f32[3,32]{1,0:T(4,128)}, u32[]{:S(2)}) copy-start(f32[3,32]{1,0:T(4,128)} %param.42) | copy-start | bytes 1156
  91.5 15.8 %copy-start.3 = (f32[561,768]{1,0:T(8,128)S(1)}, f32[561,768]{1,0:T(8,128)}, u32[]{:S(2)}) copy-start(f32[561,768]{1,0:T(8,128)} %param.23) | copy-start | bytes 5170180
  91.5 15.8 %copy-start.15 = (f32[768,192]{0,1:T(8,128)S(1)}, f32[768,192]{0,1:T(8,128)}, u32[]{:S(2)}) copy-start(f32[768,192]{0,1:T(8,128)} %param.29) | copy-start | bytes 1769476
  118.7 4.9 copy-start.12
  123.6 79.8 %copy-start.50 = (f32[768]{0:T(1024)S(1)}, f32[768]{0:T(1024)}, u32[]{:S(2)}) copy-start(f32[768]{0:T(1024)} %param.33) | copy-start | bytes 9220
  125.3 164.0 %all-reduce.12.cloned.1.call-start = ((), (), s32[]{:S(2)}) async-start(), calls=%async_computation.1 | async-start | bytes 3489792 | tf_op jit(solution)/shard_map/psum | solution.py:159
  214.8 74.5 %copy-start.51 = (f32[768]{0:T(1024)S(1)}, f32[768]{0:T(1024)}, u32[]{:S(2)}) copy-start(f32[768]{0:T(1024)} %param.39) | copy-start | bytes 9220
  214.9 162.9 %all-reduce.14.cloned.1.call-start = ((), (), s32[]{:S(2)}) async-start(), calls=%async_computation.2 | async-start | bytes 3489792 | tf_op jit(solution)/shard_map/psum | solution.py:152
  292.1 4.9 slice-start.2
  303.4 160.2 %all-reduce.16.cloned.1.call-start = ((), (), s32[]{:S(2)}) async-start(), calls=%async_computation.3 | async-start | bytes 3489792 | tf_op jit(solution)/shard_map/psum | solution.py:159
  380.1 7.0 copy-start.26
  389.2 162.0 %all-reduce.18.cloned.1.call-start = ((), (), s32[]{:S(2)}) async-start(), calls=%async_computation.4 | async-start | bytes 3489792 | tf_op jit(solution)/shard_map/psum | solution.py:244
  470.1 3.6 copy-start.42
  476.7 166.9 %all-reduce.20.cloned.1.call-start = ((), (), s32[]{:S(2)}) async-start(), calls=%async_computation.5 | async-start | bytes 3489792 | tf_op jit(solution)/shard_map/psum | solution.py:319
  551.2 5.4 slice-start
  565.2 192.7 %all-reduce.22.cloned.1.call-start = ((), (), s32[]{:S(2)}) async-start(), calls=%async_computation.6 | async-start | bytes 14155776 | tf_op jit(solution)/shard_map/psum | solution.py:339
  565.4 4.0 copy-start.45
  580.0 8.8 %copy-start.38 = (s32[561,561]{0,1:T(8,128)S(1)}, s32[561,561]{0,1:T(8,128)}, u32[]{:S(2)}) copy-start(s32[561,561]{0,1:T(8,128)} %copy-done.37) | copy-start | bytes 3776656
  588.9 14.7 %copy-start.36 = (s32[561,561]{0,1:T(8,128)S(1)}, s32[561,561]{0,1:T(8,128)}, u32[]{:S(2)}) copy-start(s32[561,561]{0,1:T(8,128)} %copy-done.35) | copy-start | bytes 3776656
  603.5 14.9 %copy-start.53 = (f32[768]{0:T(1024)S(1)}, f32[768]{0:T(1024)}, u32[]{:S(2)}) copy-start(f32[768]{0:T(1024)} %get-tuple-element.74) | copy-start | bytes 9220
  603.5 14.9 %copy-start.54 = (f32[768]{0:T(1024)S(1)}, f32[768]{0:T(1024)}, u32[]{:S(2)}) copy-start(f32[768]{0:T(1024)} %get-tuple-element.96) | copy-start | bytes 9220
  603.5 14.9 %copy-start.58 = (f32[768]{0:T(1024)S(1)}, f32[768]{0:T(1024)}, u32[]{:S(2)}) copy-start(f32[768]{0:T(1024)} %get-tuple-element.124) | copy-start | bytes 9220
  757.8 4.1 copy-start.47
  757.8 4.9 copy-start.46
  759.8 3.7 copy-start.25
  763.5 3.9 copy-start.1
  (43 other events, 70.1 us)
Sparse Core Ops, SparseCore 0:
  125.4 77.9 all-reduce.9
  215.0 74.2 all-reduce.11
  303.5 74.2 all-reduce.13
  389.3 74.2 all-reduce.15
  476.9 74.2 all-reduce.17
  565.3 74.2 all-reduce.19
  644.8 112.9 all-reduce.21
where the time goes:
time: 779 us; the launch traced here: 775 us
  waiting for transfers between devices  486 us (62%)
  matrix products  166 us (21%)
  other arithmetic  54.1 us (7%)
  local copies, waits for them, and re-layouts  27.4 us (4%)
  blocking collectives  25.3 us (3%)
  between operations  15.1 us (2%)
    psum x2, waiting for transfers between devices, forward(): branch = lax.psum(partial_value, 'narrow') + b_out  152 us
    psum x2, waiting for transfers between devices, forward(): residual_two = hidden + (lax.psum(ff_part, 'narrow') + b_down)  149 us
    psum x1, waiting for transfers between devices, local(): lax.psum((grad_w_query, grad_b_query, grad_w_key, grad_w_value, grad_b_va...  111 us
    psum x1, waiting for transfers between devices, local(): grad_hidden = grad_residual_two + lax.psum(hidden_part, 'narrow')  74.3 us
    dot_general x3, matrix products, relative_one_page(): jnp.einsum('hb,qkb->hqk', table, chooser, precision=HIGHEST, preferred_el...  73.4 us
    dot_general x3, matrix products, table_one_page(): jnp.einsum('hqk,qkb->hb', grad_page, one_hot_of(grid, bins, jnp.bfloat16)...  38.3 us
    unnamed x142, local copies, waits for them, and re-layouts  26.4 us
    psum x1, blocking collectives, local(): lax.psum((grad_w_query, grad_b_query, grad_w_key, grad_w_value, grad_b_va...  25.3 us
  transfers between devices with their start and end apart: 7, of which 6 were waited for; matrix products, arithmetic and copies ran while one was open for 7% of the time, Pallas kernels for 0%

commit v1 on v0

--- a/solution.py
+++ b/solution.py
@@ -212,8 +212,6 @@
     query_weight, key_weight, value_weight, out_weight, in_weight, down_weight = lowered
     biases = (b_query, b_value, b_out, ln1_gain, ln1_bias, b_in, b_down, ln2_gain, ln2_bias)
     output, kept_values = forward(tokens, lowered, biases, rel_bias)
-    tokens_again = lax.optimization_barrier((tokens, output))[0]
-    kept_values = forward(tokens_again, lowered, biases, rel_bias)[1]
     (
         tokens_low,
         query_rows,

time: 779 us -> 595 us (0.76)
  waiting for transfers between devices: 486 us -> 337 us
  matrix products: 166 us -> 146 us
  other arithmetic: 54.1 us -> 44.4 us
    psum x2 -> x1, waiting for transfers between devices: 149 us -> 74.2 us  [forward(): residual_two = hidden + (lax.psum(ff_part, 'narrow') + b_down)]
    psum x2 -> x1, waiting for transfers between devices: 152 us -> 78 us  [forward(): branch = lax.psum(partial_value, 'narrow') + b_out]
    dot_general x2 -> x1, matrix products: 11 us -> 2.06 us  [forward(): ff_part = jnp.dot(active, down_weight, preferred_element_type=jnp.float32)]
    unnamed x142 -> x134, local copies, waits for them, and re-layouts: 26.4 us -> 21.7 us
  transfers between devices with their start and end apart: 7 -> 5, of which waited for: 6 -> 4; matrix products, arithmetic and copies ran while one was open for 7% -> 9% of each run, Pallas kernels for 0% -> 0%
where the time goes in v1:
time: 595 us; the launch traced here: 590 us
  waiting for transfers between devices  337 us (57%)
  matrix products  146 us (25%)
  other arithmetic  44.4 us (7%)
  blocking collectives  25.3 us (4%)
  local copies, waits for them, and re-layouts  21.8 us (4%)
  between operations  14.8 us (2%)
    psum x1, waiting for transfers between devices, local(): lax.psum((grad_w_query, grad_b_query, grad_w_key, grad_w_value, grad_b_va...  110 us
    psum x1, waiting for transfers between devices, forward(): branch = lax.psum(partial_value, 'narrow') + b_out  78 us
    psum x1, waiting for transfers between devices, local(): grad_hidden = grad_residual_two + lax.psum(hidden_part, 'narrow')  74.4 us
    psum x1, waiting for transfers between devices, forward(): residual_two = hidden + (lax.psum(ff_part, 'narrow') + b_down)  74.2 us
    dot_general x3, matrix products, relative_one_page(): jnp.einsum('hb,qkb->hqk', table, chooser, precision=HIGHEST, preferred_el...  70.8 us
    dot_general x3, matrix products, table_one_page(): jnp.einsum('hqk,qkb->hb', grad_page, one_hot_of(grid, bins, jnp.bfloat16)...  38.3 us
    psum x1, blocking collectives, local(): lax.psum((grad_w_query, grad_b_query, grad_w_key, grad_w_value, grad_b_va...  25.3 us
    unnamed x134, local copies, waits for them, and re-layouts  21.7 us
  transfers between devices with their start and end apart: 5, of which 4 were waited for; matrix products, arithmetic and copies ran while one was open for 9% of the time, Pallas kernels for 0%

profile of v1, /device:TPU:0, one launch (start us, length us, event | category | flops | bytes accessed | tf_op | source)
XLA Modules:
  0.0 590.3 jit_solution(837161568791828724)
XLA Ops:
  7.3 1.6 convert_element_type.909
  9.0 13.5 %fusion.104 = s32[561]{0:T(1024)S(1)} fusion(s32[561]{0:T(1024)S(1)} %copy-done.47), kind=kLoop, calls=%fused_computation.156 | loop fusion | flops 943602 | bytes 4488 | tf_op jit(solution)/shard_map/reduce_sum | solution.py:63
  22.5 2.5 convert_add_fusion.2
  26.0 9.5 %convert_add_fusion = (s32[561,561]{0,1:T(8,128)S(1)}, s32[561,561]{0,1:T(8,128)S(1)}) fusion(s32[561]{0:T(1024)S(1)} %get-tuple-element.75, s32[561]{0:T(1024)S(1)} %get-tuple-element.74), kind=kLoop, calls=%fused_computation.153 | loop fusion | flops 61055736 | bytes 2522256 | tf_op jit(solution)/shard_map/while/body/eval_jaxpr/add | solution.py:46
  35.6 28.1 %fusion.1 = f32[561,561,3]{0,2,1:T(4,128)S(1)} fusion(s32[561,561]{0,1:T(8,128)S(1)} %get-tuple-element.121, f32[3,64]{1,0:T(4,128)S(1)} %copy-done), kind=kOutput, calls=%fused_computation.2 | convolution fusion | flops 745259328 | bytes 5036304 | tf_op jit(solution)/shard_map/while/body/eval_jaxpr/hb,qkb->hqk/dot_general | solution.py:84
  63.7 28.5 %fusion.3 = f32[561,561,3]{0,2,1:T(4,128)S(1)} fusion(s32[561,561]{0,1:T(8,128)S(1)} %get-tuple-element.122, f32[3,64]{1,0:T(4,128)S(1)} %copy-done.58), kind=kOutput, calls=%fused_computation.5 | convolution fusion | flops 745259328 | bytes 5036304 | tf_op jit(solution)/shard_map/while/body/eval_jaxpr/hb,qkb->hqk/dot_general | solution.py:84
  92.2 14.3 %fusion.9 = f32[561,561,3]{0,2,1:T(4,128)S(1)} fusion(s32[561,561]{0,1:T(8,128)S(1)} %convert_add_fusion.2, f32[3,32]{1,0:T(4,128)S(1)} %copy-done.59), kind=kOutput, calls=%fused_computation.12 | convolution fusion | flops 372629664 | bytes 5035920 | tf_op jit(solution)/shard_map/while/body/eval_jaxpr/hb,qkb->hqk/dot_general | solution.py:84
  106.5 2.3 fusion.156
  112.5 1.6 fusion.133
  114.2 78.0 %all-reduce.8.cloned.1.call-done = f32[561,768]{1,0:T(8,128)} async-done(((f32[561,768]{1,0:T(8,128)}), f32[561,768]{1,0:T(8,128)}) %all-reduce.8.cloned.1.call-update) | async-done | bytes 1723408 | tf_op jit(solution)/shard_map/psum | solution.py:152
  192.3 2.4 fusion.155
  195.5 6.0 %multiply_convert_fusion.1 = (bf16[561,768]{1,0:T(8,128)(2,1)S(1)}, f32[561,768]{1,0:T(8,128)}, f32[561,768]{1,0:T(8,128)}) fusion(f32[768]{0:T(1024)S(1)} %copy-done.57, f32[768,768]{1,0:T(8,128)S(1)} %copy-done.20, f32[561,768]{1,0:T(8,128)S(1)} %get-tuple-element.108, f32[768]{0:T(1024)S(1)} %copy-done.52, f32[768]{0:T(1024)S(1)} %copy-done.46, ...), kind=kOutput, calls=%fused_computation.131 | convolution fusion | flops 692962560 | bytes 8404872 | tf_op jit(solution)/shard_map/dot_general | solution.py:156
  202.4 2.1 fusion.125
  204.8 74.2 %all-reduce.10.cloned.1.call-done = f32[561,768]{1,0:T(8,128)} async-done(((f32[561,768]{1,0:T(8,128)}), f32[561,768]{1,0:T(8,128)}) %all-reduce.10.cloned.1.call-update) | async-done | bytes 1723408 | tf_op jit(solution)/shard_map/psum | solution.py:159
  278.9 2.1 fusion.153
  283.3 1.9 fusion.152
  285.9 2.1 copy-done.19
  290.3 2.1 fusion.129
  292.5 74.4 %all-reduce.12.cloned.1.call-done = f32[561,768]{1,0:T(8,128)} async-done(((f32[561,768]{1,0:T(8,128)}), f32[561,768]{1,0:T(8,128)}) %all-reduce.12.cloned.1.call-update) | async-done | bytes 1723408 | tf_op jit(solution)/shard_map/psum | solution.py:242
  366.9 3.1 multiply_reduce_fusion.2
  379.7 1.7 add_add_fusion.2
  381.9 4.0 fusion.158
  385.9 2.9 fusion.148
  389.0 2.2 fusion.157
  396.5 8.8 %fusion.114 = f32[3,32]{1,0:T(4,128)S(1)} fusion(s32[561,561]{0,1:T(8,128)} %copy-done.32, bf16[3,561,561]{1,2,0:T(8,128)(2,1)S(1)} %copy-done.4), kind=kOutput, calls=%fused_computation.173 | convolution fusion | flops 70497504 | bytes 3147594 | tf_op jit(solution)/shard_map/while/body/eval_jaxpr/hqk,qkb->hb/dot_general | solution.py:100
  405.4 14.6 %fusion.117 = f32[3,64]{1,0:T(4,128)S(1)} fusion(s32[561,561]{0,1:T(8,128)S(1)} %copy-done.36, bf16[3,561,561]{1,2,0:T(8,128)(2,1)S(1)} %copy-done.4), kind=kOutput, calls=%fused_computation.174 | convolution fusion | flops 140995008 | bytes 3147978 | tf_op jit(solution)/shard_map/while/body/eval_jaxpr/hqk,qkb->hb/dot_general | solution.py:100
  420.0 14.8 %fusion.120 = f32[3,64]{1,0:T(4,128)S(1)} fusion(s32[561,561]{0,1:T(8,128)S(1)} %copy-done.34, bf16[3,561,561]{1,2,0:T(8,128)(2,1)S(1)} %copy-done.4), kind=kOutput, calls=%fused_computation.175 | convolution fusion | flops 140995008 | bytes 3147978 | tf_op jit(solution)/shard_map/while/body/eval_jaxpr/hqk,qkb->hb/dot_general | solution.py:100
  434.8 25.3 %all-reduce = (f32[192]{0:T(256)}, f32[192]{0:T(256)}, f32[768]{0:T(1024)}, f32[768]{0:T(1024)}, f32[768]{0:T(1024)}, /*index=5*/f32[768]{0:T(1024)}, f32[768]{0...) all-reduce(f32[192]{0:T(256)S(1)} %reduce_sum.203, ...), channel_id=1, replica_groups=mesh['wide'=8,'narrow'=4] {'wide'}, use_global_device_ids=true, to_apply=%region_18.19 | all-reduce | flops 6240 | bytes 49920 | tf_op jit(solution)/shard_map/psum | solution.py:337
  460.1 3.4 add_add_fusion.5
  463.5 110.4 %all-reduce.16.cloned.1.call-done = (f32[768,192]{0,1:T(8,128)}, f32[768,192]{0,1:T(8,128)}, f32[768,192]{0,1:T(8,128)}, f32[192,768]{1,0:T(8,128)}, f32[768,768]{1,0:T(8,128)}, /*index=5*/f32[768,768]{1,0:T(8,128)}) async-done(((f32[768,192]{0,1:T(8,128)}, f32[768,192]{0,1:T(8,128)}, f32[768,192]{0,1:T(8,128)}, f32[192,768]{1,0:T(8,128)}, f32[768,768]{1,0:T(8,128)}, /*index=5*/f32[768,768]{1,0:T(8,128)}), ...) | async-done | bytes 7077904 | tf_op jit(solution)/shard_map/psum | solution.py:337
  573.9 2.0 copy.111
  575.9 2.1 copy.112
  (179 shorter events, 33.0 us)
Async XLA Ops:
  7.2 28.4 %copy-start = (f32[3,64]{1,0:T(4,128)S(1)}, f32[3,64]{1,0:T(4,128)}, u32[]{:S(2)}) copy-start(f32[3,64]{1,0:T(4,128)} %param.44) | copy-start | bytes 2308
  7.2 15.2 %copy-start.53 = (s32[561]{0:T(1024)S(1)}, s32[561]{0:T(1024)}, u32[]{:S(2)}) copy-start(s32[561]{0:T(1024)} %param.25) | copy-start | bytes 6736
  7.2 17.7 %copy-start.12 = (f32[768,192]{0,1:T(8,128)S(1)}, f32[768,192]{0,1:T(8,128)}, u32[]{:S(2)}) copy-start(f32[768,192]{0,1:T(8,128)} %param.29) | copy-start | bytes 1769476
  7.2 185.0 %all-reduce.8.cloned.1.call-start = ((), (), s32[]{:S(2)}) async-start(), calls=%async_computation | async-start | bytes 3489792 | tf_op jit(solution)/shard_map/psum | solution.py:152
  8.9 16.5 %copy-start.16 = (f32[768,192]{0,1:T(8,128)S(1)}, f32[768,192]{0,1:T(8,128)}, u32[]{:S(2)}) copy-start(f32[768,192]{0,1:T(8,128)} %param.27) | copy-start | bytes 1769476
  8.9 16.5 %copy-start.55 = (f32[192]{0:T(256)S(1)}, f32[192]{0:T(256)}, u32[]{:S(2)}) copy-start(f32[192]{0:T(256)} %param.28) | copy-start | bytes 2308
  25.0 67.2 %copy-start.32 = (s32[561,561]{0,1:T(8,128)}, s32[561,561]{0,1:T(8,128)S(1)}, u32[]{:S(2)}) copy-start(s32[561,561]{0,1:T(8,128)S(1)} %convert_add_fusion.2) | copy-start | bytes 3776656
  25.5 81.0 %copy-start.24 = (bf16[561,192]{0,1:T(8,128)(2,1)}, bf16[561,192]{0,1:T(8,128)(2,1)S(1)}, u32[]{:S(2)}) copy-start(bf16[561,192]{0,1:T(8,128)(2,1)S(1)} %convolution_convert_fusion.1) | copy-start | bytes 646276
  26.0 80.5 %copy-start.22 = (bf16[561,192]{0,1:T(8,128)(2,1)}, bf16[561,192]{0,1:T(8,128)(2,1)S(1)}, u32[]{:S(2)}) copy-start(bf16[561,192]{0,1:T(8,128)(2,1)S(1)} %fusion.112) | copy-start | bytes 646276
  35.6 28.1 %copy-start.33 = (s32[561,561]{0,1:T(8,128)}, s32[561,561]{0,1:T(8,128)S(1)}, u32[]{:S(2)}) copy-start(s32[561,561]{0,1:T(8,128)S(1)} %get-tuple-element.121) | copy-start | bytes 3776656
  35.6 28.1 %copy-start.35 = (s32[561,561]{0,1:T(8,128)}, s32[561,561]{0,1:T(8,128)S(1)}, u32[]{:S(2)}) copy-start(s32[561,561]{0,1:T(8,128)S(1)} %get-tuple-element.122) | copy-start | bytes 3776656
  35.6 28.1 %copy-start.58 = (f32[3,64]{1,0:T(4,128)S(1)}, f32[3,64]{1,0:T(4,128)}, u32[]{:S(2)}) copy-start(f32[3,64]{1,0:T(4,128)} %param.43) | copy-start | bytes 2308
  63.7 28.5 %copy-start.59 = (f32[3,32]{1,0:T(4,128)S(1)}, f32[3,32]{1,0:T(4,128)}, u32[]{:S(2)}) copy-start(f32[3,32]{1,0:T(4,128)} %param.42) | copy-start | bytes 1156
  112.5 79.8 %copy-start.50 = (f32[768]{0:T(1024)S(1)}, f32[768]{0:T(1024)}, u32[]{:S(2)}) copy-start(f32[768]{0:T(1024)} %param.33) | copy-start | bytes 9220
  114.2 164.7 %all-reduce.10.cloned.1.call-start = ((), (), s32[]{:S(2)}) async-start(), calls=%async_computation.1 | async-start | bytes 3489792 | tf_op jit(solution)/shard_map/psum | solution.py:159
  195.5 6.9 %copy-start.18 = (f32[768,768]{1,0:T(8,128)S(1)}, f32[768,768]{1,0:T(8,128)}, u32[]{:S(2)}) copy-start(f32[768,768]{1,0:T(8,128)} %param.38) | copy-start | bytes 7077892
  204.5 74.5 %copy-start.51 = (f32[768]{0:T(1024)S(1)}, f32[768]{0:T(1024)}, u32[]{:S(2)}) copy-start(f32[768]{0:T(1024)} %param.39) | copy-start | bytes 9220
  204.5 162.4 %all-reduce.12.cloned.1.call-start = ((), (), s32[]{:S(2)}) async-start(), calls=%async_computation.2 | async-start | bytes 3489792 | tf_op jit(solution)/shard_map/psum | solution.py:242
  285.2 4.1 copy-start.6
  285.5 3.9 copy-start.40
  292.4 167.6 %all-reduce.14.cloned.1.call-start = ((), (), s32[]{:S(2)}) async-start(), calls=%async_computation.3 | async-start | bytes 3489792 | tf_op jit(solution)/shard_map/psum | solution.py:317
  366.9 5.9 slice-start
  373.7 5.8 copy-start.26
  381.4 192.5 %all-reduce.16.cloned.1.call-start = ((), (), s32[]{:S(2)}) async-start(), calls=%async_computation.4 | async-start | bytes 14155776 | tf_op jit(solution)/shard_map/psum | solution.py:337
  381.9 4.1 copy-start.43
  388.8 3.6 copy-start.29
  396.5 8.8 %copy-start.36 = (s32[561,561]{0,1:T(8,128)S(1)}, s32[561,561]{0,1:T(8,128)}, u32[]{:S(2)}) copy-start(s32[561,561]{0,1:T(8,128)} %copy-done.35) | copy-start | bytes 3776656
  405.4 14.7 %copy-start.34 = (s32[561,561]{0,1:T(8,128)S(1)}, s32[561,561]{0,1:T(8,128)}, u32[]{:S(2)}) copy-start(s32[561,561]{0,1:T(8,128)} %copy-done.33) | copy-start | bytes 3776656
  573.9 4.1 copy-start.45
  573.9 4.9 copy-start.44
  575.9 3.7 copy-start.15
  579.6 3.9 copy-start.1
  (37 other events, 59.5 us)
Sparse Core Ops, SparseCore 0:
  114.3 77.9 all-reduce.7
  204.6 74.2 all-reduce.9
  292.6 74.2 all-reduce.11
  381.5 74.2 all-reduce.13
  460.9 112.9 all-reduce.15

commit v2 on v1

--- a/solution.py
+++ b/solution.py
@@ -3,6 +3,8 @@
 import jax
 import jax.numpy as jnp
 from jax import lax
+from jax.experimental import pallas as pl
+from jax.experimental.pallas import tpu as pltpu
 from jax.sharding import PartitionSpec as P
 
 HEAD_DIM = 64
@@ -47,6 +49,272 @@
     return result
 
 
+MESH = pl.DeviceIdType.MESH
+CH = 96
+PC = 48
+
+
+def erf_of(x):
+    x = jnp.clip(x, -3.832506856900711, 3.832506856900711)
+    s = x * x
+    top = -2.72614225801306e-10
+    for term in (2.77068142495902e-08, -2.10102402082508e-06, -5.69250639462346e-05,
+                 -7.34990630326855e-04, -2.95459980854025e-03, -1.60960333262415e-02):
+        top = top * s + term
+    low = -1.45660718464996e-05
+    for term in (-2.13374055278905e-04, -1.68282697438203e-03, -7.37332916720468e-03,
+                 -1.42647390514189e-02):
+        low = low * s + term
+    return x * top / low
+
+
+def normal_cdf(x):
+    return 0.5 + 0.5 * erf_of(x * math.sqrt(0.5))
+
+
+def centre(values):
+    c = values - jnp.mean(values, axis=-1, keepdims=True)
+    r = lax.rsqrt(jnp.mean(c * c, axis=-1, keepdims=True) + EPSILON)
+    return c * r, r
+
+
+def norm_back(g, n, r, gain):
+    m = g * gain
+    return r * (m - jnp.mean(m, axis=-1, keepdims=True) - n * jnp.mean(m * n, axis=-1, keepdims=True))
+
+
+def dot_nn(a, b):
+    return lax.dot_general(a, b, (((1,), (0,)), ((), ())), preferred_element_type=jnp.float32)
+
+
+def dot_nt(a, b):
+    return lax.dot_general(a, b, (((1,), (1,)), ((), ())), preferred_element_type=jnp.float32)
+
+
+def dot_tn(a, b):
+    return lax.dot_general(a, b, (((0,), (0,)), ((), ())), preferred_element_type=jnp.float32)
+
+
+class LineSum:
+    def __init__(self, part, rx_in, rx_mid, tot, s_in, s_mid, r_in, r_mid):
+        self.part, self.rx_in, self.rx_mid, self.tot = part, rx_in, rx_mid, tot
+        self.s_in, self.s_mid, self.r_in, self.r_mid = s_in, s_mid, r_in, r_mid
+        w, n = lax.axis_index("wide"), lax.axis_index("narrow")
+        self.end = (n == 0) | (n == 3)
+        self.mid = jnp.logical_not(self.end)
+        self.side = (w, n + 1 - 2 * lax.rem(n, 2))
+        self.across = (w, 3 - n)
+        self.pieces = part.shape[0] // PC
+
+    def rows(self, p):
+        return pl.ds(pl.multiple_of(p * PC, PC), PC)
+
+    def copy_a(self, p):
+        return pltpu.make_async_remote_copy(self.part.at[self.rows(p)], self.rx_in.at[self.rows(p)],
+            self.s_in.at[p], self.r_in.at[p], device_id=self.side, device_id_type=MESH)
+
+    def copy_b(self, p):
+        return pltpu.make_async_remote_copy(self.part.at[self.rows(p)], self.rx_mid.at[self.rows(p)],
+            self.s_mid.at[p], self.r_mid.at[p], device_id=self.across, device_id_type=MESH)
+
+    def copy_t(self, p):
+        return pltpu.make_async_remote_copy(self.tot.at[self.rows(p)], self.tot.at[self.rows(p)],
+            self.s_in.at[p], self.r_in.at[p], device_id=self.side, device_id_type=MESH)
+
+    def barrier(self):
+        bar = pltpu.get_barrier_semaphore()
+        pl.semaphore_signal(bar, inc=1, device_id=self.side, device_id_type=MESH)
+
+        @pl.when(self.mid)
+        def _():
+            pl.semaphore_signal(bar, inc=1, device_id=self.across, device_id_type=MESH)
+
+        @pl.when(self.end)
+        def _():
+            pl.semaphore_wait(bar, 1)
+
+        @pl.when(self.mid)
+        def _():
+            pl.semaphore_wait(bar, 2)
+
+    def free_part(self, p):
+        @pl.when(self.end)
+        def _():
+            self.copy_a(p).wait_send()
+
+        @pl.when(self.mid)
+        def _():
+            self.copy_b(p).wait_send()
+
+    def finish(self, p, first):
+        self.copy_b(p).wait_recv()
+        if not first:
+            self.copy_t(p).wait_send()
+        self.tot[self.rows(p), :] = self.part[self.rows(p), :] + self.rx_mid[self.rows(p), :]
+        self.copy_t(p).start()
+
+    def slot(self, p, order):
+        @pl.when(self.end)
+        def _():
+            self.copy_a(p).start()
+
+        @pl.when(self.mid)
+        def _():
+            self.copy_a(p).wait_recv()
+            self.part[self.rows(p), :] += self.rx_in[self.rows(p), :]
+            self.copy_b(p).start()
+
+            @pl.when(p > 0)
+            def _():
+                self.finish(p - 1, order == 0)
+
+            if order > 0:
+                @pl.when(p == 0)
+                def _():
+                    self.finish(self.pieces - 1, order == 1)
+
+    def last(self, first):
+        @pl.when(self.mid)
+        def _():
+            self.finish(self.pieces - 1, first)
+
+    def want(self, p):
+        @pl.when(self.end)
+        def _():
+            self.copy_t(p).wait_recv()
+
+    def drain(self):
+        def one(p, c):
+            self.free_part(p)
+
+            @pl.when(self.mid)
+            def _():
+                self.copy_t(p).wait_send()
+            return c
+        lax.fori_loop(0, self.pieces, one, 0)
+
+
+def middle_kernel(tok_ref, cot_ref, att_ref, w_out_ref, w_in_ref, w_down_ref, vec_ref,
+                  out_ref, gres_ref, dwin_ref, dwdown_ref, small_ref,
+                  part, rx_in, rx_mid, tot, res, hid, pre, act, gff, hlow, gpre, wo, wi, wd,
+                  s_in, s_mid, r_in, r_mid):
+    line = LineSum(part, rx_in, rx_mid, tot, s_in, s_mid, r_in, r_mid)
+    steps = part.shape[0] // CH
+    k = CH // PC
+    b_out, g1, b1, b_in = (vec_ref[i:i + 1, :] for i in range(4))
+    b_down, g2, b2 = (vec_ref[i:i + 1, :] for i in range(4, 7))
+    wo[...] = w_out_ref[...].astype(jnp.bfloat16)
+    line.barrier()
+
+    def rows(c):
+        return pl.ds(pl.multiple_of(c * CH, CH), CH)
+
+    def branch_step(c, carry):
+        r = rows(c)
+        part[r, :] = dot_nn(att_ref[r, :], wo[...])
+        for j in range(k):
+            line.slot(c * k + j, 0)
+        return carry
+    lax.fori_loop(0, steps, branch_step, 0)
+    wi[...] = w_in_ref[...].astype(jnp.bfloat16)
+    wd[...] = w_down_ref[...].astype(jnp.bfloat16)
+    small_ref[...] = jnp.zeros_like(small_ref)
+
+    def open_step(c):
+        for j in range(k):
+            line.want(c * k + j)
+        for j in range(k):
+            line.free_part(c * k + j)
+
+    def forward_step(c, carry):
+        r = rows(c)
+        open_step(c)
+        one = tok_ref[r, :] + (tot[r, :] + b_out)
+        res[r, :] = one
+        n, _ = centre(one)
+        hidden = n * g1 + b1
+        hid[r, :] = hidden
+        low = hidden.astype(jnp.bfloat16)
+        hlow[r, :] = low
+        u = dot_nn(low, wi[...]) + b_in
+        pre[r, :] = u
+        a = (u * normal_cdf(u)).astype(jnp.bfloat16)
+        act[r, :] = a
+        part[r, :] = dot_nn(a, wd[...])
+        for j in range(k):
+            line.slot(c * k + j, 1)
+        return carry
+    lax.fori_loop(0, steps, forward_step, 0)
+
+    def add_row(i, rows_value):
+        small_ref[i:i + 1, :] += jnp.sum(rows_value, axis=0, keepdims=True)
+
+    def back_step(c, carry):
+        r = rows(c)
+        open_step(c)
+        two = hid[r, :] + (tot[r, :] + b_down)
+        n, rs = centre(two)
+        out_ref[r, :] = n * g2 + b2
+        g = cot_ref[r, :]
+        add_row(0, g * n)
+        add_row(1, g)
+        back = norm_back(g, n, rs, g2)
+        hid[r, :] = back
+        low = back.astype(jnp.bfloat16)
+        gff[r, :] = low
+        add_row(2, low.astype(jnp.float32))
+        ga = dot_nt(low, wd[...])
+        u = pre[r, :]
+        slope = normal_cdf(u) + u * (jnp.exp(-0.5 * u * u) * (1.0 / math.sqrt(2.0 * math.pi)))
+        gp = (ga * slope).astype(jnp.bfloat16)
+        gpre[r, :] = gp
+        add_row(3, gp.astype(jnp.float32))
+        part[r, :] = dot_nt(gp, wi[...])
+        for j in range(k):
+            line.slot(c * k + j, 2)
+        return carry
+    lax.fori_loop(0, steps, back_step, 0)
+    line.last(False)
+    dwdown_ref[...] = dot_tn(act[...], gff[...])
+    dwin_ref[...] = dot_tn(hlow[...], gpre[...])
+
+    def close_step(c, carry):
+        r = rows(c)
+        for j in range(k):
+            line.want(c * k + j)
+        g = hid[r, :] + tot[r, :]
+        n, rs = centre(res[r, :])
+        add_row(4, g * n)
+        add_row(5, g)
+        back = norm_back(g, n, rs, g1)
+        gres_ref[r, :] = back
+        add_row(6, back.astype(jnp.bfloat16).astype(jnp.float32))
+        return carry
+    lax.fori_loop(0, steps, close_step, 0)
+    line.drain()
+
+
+def middle(tok, cot, att, w_out, w_in, w_down, vec):
+    rows, d = tok.shape
+    heads, f = w_out.shape[0], w_in.shape[1]
+    pieces = rows // PC
+    f32, bf = jnp.float32, jnp.bfloat16
+    shapes = (jax.ShapeDtypeStruct((rows, d), f32), jax.ShapeDtypeStruct((rows, d), f32),
+              jax.ShapeDtypeStruct((d, f), f32), jax.ShapeDtypeStruct((f, d), f32),
+              jax.ShapeDtypeStruct((8, d), f32))
+    vm = pl.BlockSpec(memory_space=pltpu.VMEM)
+    big = [pltpu.VMEM((rows, d), f32) for _ in range(6)]
+    return pl.pallas_call(
+        middle_kernel, out_shape=shapes, in_specs=[vm] * 7, out_specs=[vm] * 5,
+        scratch_shapes=big + [pltpu.VMEM((rows, f), f32), pltpu.VMEM((rows, f), bf), pltpu.VMEM((rows, d), bf),
+                              pltpu.VMEM((rows, d), bf), pltpu.VMEM((rows, f), bf),
+                              pltpu.VMEM((heads, d), bf), pltpu.VMEM((d, f), bf), pltpu.VMEM((f, d), bf)]
+        + [pltpu.SemaphoreType.DMA((pieces,))] * 4,
+        compiler_params=pltpu.CompilerParams(collective_id=0, has_side_effects=True, vmem_limit_bytes=56 << 20),
+        cost_estimate=pl.CostEstimate(flops=6 * 2 * rows * d * f, bytes_accessed=20 << 20, transcendentals=rows * f),
+    )(tok, cot, att, w_out, w_in, w_down, vec)
+
+
 def norm_layer(values, gain_row, shift_row):
     average = jnp.mean(values, axis=-1, keepdims=True)
     centred = values - average
@@ -148,30 +416,7 @@
         preferred_element_type=jnp.float32,
     )
     attended = mixed.reshape(tokens.shape[0], -1).astype(jnp.bfloat16)
-    partial_value = jnp.dot(attended, out_weight, preferred_element_type=jnp.float32)
-    branch = lax.psum(partial_value, "narrow") + b_out
-    residual_one = tokens + branch
-    hidden = norm_layer(residual_one, ln1_gain, ln1_bias)
-    hidden_low = hidden.astype(jnp.bfloat16)
-    pre_gelu = jnp.dot(hidden_low, in_weight, preferred_element_type=jnp.float32) + b_in
-    active = gelu_exact(pre_gelu).astype(jnp.bfloat16)
-    ff_part = jnp.dot(active, down_weight, preferred_element_type=jnp.float32)
-    residual_two = hidden + (lax.psum(ff_part, "narrow") + b_down)
-    output = norm_layer(residual_two, ln2_gain, ln2_bias)
-    kept_values = (
-        tokens_low,
-        query_rows,
-        key_rows,
-        value_rows,
-        log_total,
-        attended,
-        residual_one,
-        hidden_low,
-        pre_gelu,
-        active,
-        residual_two,
-    )
-    return (output, kept_values)
+    return tokens_low, query_rows, key_rows, value_rows, log_total, attended
 
 
 def local(
@@ -211,39 +456,18 @@
     )
     query_weight, key_weight, value_weight, out_weight, in_weight, down_weight = lowered
     biases = (b_query, b_value, b_out, ln1_gain, ln1_bias, b_in, b_down, ln2_gain, ln2_bias)
-    output, kept_values = forward(tokens, lowered, biases, rel_bias)
-    (
-        tokens_low,
-        query_rows,
-        key_rows,
-        value_rows,
-        log_total,
-        attended,
-        residual_one,
-        hidden_low,
-        pre_gelu,
-        active,
-        residual_two,
-    ) = kept_values
+    tokens_low, query_rows, key_rows, value_rows, log_total, attended = forward(tokens, lowered, biases, rel_bias)
+    extra = -length % 64
+    pad = ((0, extra), (0, 0))
+    vec = jnp.stack([b_out, ln1_gain, ln1_bias, b_in, b_down, ln2_gain, ln2_bias, b_down])
+    output, grad_residual_one, grad_w_in, grad_w_down, small = middle(
+        jnp.pad(tokens, pad), jnp.pad(cotangent, pad), jnp.pad(attended, pad), w_out, w_in, w_down, vec)
+    output, grad_residual_one = output[:length], grad_residual_one[:length]
+    grad_ln2_gain, grad_ln2_bias, grad_b_down, grad_b_in, grad_ln1_gain, grad_ln1_bias, grad_b_out = (small[i] for i in range(7))
     head_count = rel_bias.shape[1]
     shape_heads = (page_count, length, head_count, HEAD_DIM)
     head_width = head_count * HEAD_DIM
-    _, second_back = jax.vjp(norm_layer, residual_two, ln2_gain, ln2_bias)
-    grad_residual_two, grad_ln2_gain, grad_ln2_bias = second_back(cotangent)
-    grad_ff = grad_residual_two.astype(jnp.bfloat16)
-    grad_b_down = jnp.sum(grad_ff, axis=0, dtype=jnp.float32)
-    grad_w_down = jnp.einsum("tf,td->fd", active, grad_ff, preferred_element_type=jnp.float32)
-    grad_active = jnp.einsum("td,fd->tf", grad_ff, down_weight, preferred_element_type=jnp.float32)
-    _, gelu_back = jax.vjp(gelu_exact, pre_gelu)
-    grad_pre = gelu_back(grad_active)[0].astype(jnp.bfloat16)
-    grad_b_in = jnp.sum(grad_pre, axis=0, dtype=jnp.float32)
-    grad_w_in = jnp.einsum("td,tf->df", hidden_low, grad_pre, preferred_element_type=jnp.float32)
-    hidden_part = jnp.einsum("tf,df->td", grad_pre, in_weight, preferred_element_type=jnp.float32)
-    grad_hidden = grad_residual_two + lax.psum(hidden_part, "narrow")
-    _, first_back = jax.vjp(norm_layer, residual_one, ln1_gain, ln1_bias)
-    grad_residual_one, grad_ln1_gain, grad_ln1_bias = first_back(grad_hidden)
     grad_branch = grad_residual_one.astype(jnp.bfloat16)
-    grad_b_out = jnp.sum(grad_branch, axis=0, dtype=jnp.float32)
     grad_w_out = jnp.einsum("tc,td->cd", attended, grad_branch, preferred_element_type=jnp.float32)
     grad_attended = jnp.einsum(
         "td,cd->tc", grad_branch, out_weight, preferred_element_type=jnp.float32

time: 595 us -> 479 us (0.81)
  waiting for transfers between devices: 337 us -> 116 us
  Pallas kernels: 0 us -> 138 us
  matrix products: 146 us -> 127 us
  other arithmetic: 44.4 us -> 32.1 us
    psum x3 -> x0, waiting for transfers between devices: 227 us -> none  [the longest x1 78 us: forward(): branch = lax.psum(partial_value, 'narrow') + b_out]
    pallas_call x0 -> x1, Pallas kernels: none -> 138 us  [middle(): pl.pallas_call(middle_kernel, out_shape=shapes, in_specs=[vm] * 7, out_sp...]
    dot_general x7 -> x0, matrix products: 20.1 us -> none  [the longest x1 5.98 us: forward(): jnp.dot(hidden_low, in_weight, preferred_element_type=jnp.float32) + b_in]
    reduce_sum x10 -> x0, other arithmetic: 12.2 us -> none  [the longest x2 4.53 us: norm_layer(): average = jnp.mean(values, axis=-1, keepdims=True)]
    unnamed x134 -> x108, local copies, waits for them, and re-layouts: 21.7 us -> 13.1 us
  transfers between devices with their start and end apart: 5 -> 2, of which waited for: 4 -> 2; matrix products, arithmetic and copies ran while one was open for 9% -> 10% of each run, Pallas kernels for 0% -> 0%
where the time goes in v2:
time: 479 us; the launch traced here: 475 us
  Pallas kernels  138 us (29%)
  matrix products  127 us (27%)
  waiting for transfers between devices  116 us (24%)
  other arithmetic  32.1 us (7%)
  blocking collectives  24.9 us (5%)
  local copies, waits for them, and re-layouts  21.4 us (4%)
  between operations  15.2 us (3%)
    pallas_call x1, Pallas kernels, middle(): pl.pallas_call(middle_kernel, out_shape=shapes, in_specs=[vm] * 7, out_sp...  138 us
    psum x1, waiting for transfers between devices, local(): lax.psum((grad_w_query, grad_b_query, grad_w_key, grad_w_value, grad_b_va...  115 us
    dot_general x3, matrix products, relative_one_page(): jnp.einsum('hb,qkb->hqk', table, chooser, precision=HIGHEST, preferred_el...  70.8 us
    dot_general x3, matrix products, table_one_page(): jnp.einsum('hqk,qkb->hb', grad_page, one_hot_of(grid, bins, jnp.bfloat16)...  37.4 us
    psum x1, blocking collectives, local(): lax.psum((grad_w_query, grad_b_query, grad_w_key, grad_w_value, grad_b_va...  24.9 us
    reduce_sum x1, other arithmetic, reading_place(): return (jnp.sum(earlier, axis=2) + order_rank).astype(jnp.int32)  13.4 us
    unnamed x108, local copies, waits for them, and re-layouts  13.1 us
    add x2, other arithmetic, bucket_of(): result = result + (magnitude >= level_start).astype(jnp.int32)  12 us
  transfers between devices with their start and end apart: 2, of which 2 were waited for; matrix products, arithmetic and copies ran while one was open for 10% of the time, Pallas kernels for 0%

profile of v2, /device:TPU:0, one launch (start us, length us, event | category | flops | bytes accessed | tf_op | source)
XLA Modules:
  0.0 475.0 jit_solution(1623799645359743388)
XLA Ops:
  7.3 1.6 convert_element_type.887
  9.0 13.4 %fusion.99 = s32[561]{0:T(1024)S(1)} fusion(s32[561]{0:T(1024)S(1)} %copy-done.35), kind=kLoop, calls=%fused_computation.121 | loop fusion | flops 943602 | bytes 4488 | tf_op jit(solution)/shard_map/reduce_sum | solution.py:331
  22.4 2.5 convert_add_fusion.2
  25.9 9.5 %convert_add_fusion = (s32[561,561]{0,1:T(8,128)S(1)}, s32[561,561]{0,1:T(8,128)S(1)}) fusion(s32[561]{0:T(1024)S(1)} %get-tuple-element.86, s32[561]{0:T(1024)S(1)} %get-tuple-element.85), kind=kLoop, calls=%fused_computation.118 | loop fusion | flops 61055736 | bytes 2522256 | tf_op jit(solution)/shard_map/while/body/eval_jaxpr/add | solution.py:48
  35.5 28.1 %fusion.1 = f32[561,561,3]{0,2,1:T(4,128)S(1)} fusion(s32[561,561]{0,1:T(8,128)S(1)} %get-tuple-element.113, f32[3,64]{1,0:T(4,128)S(1)} %copy-done), kind=kOutput, calls=%fused_computation.2 | convolution fusion | flops 745259328 | bytes 5036304 | tf_op jit(solution)/shard_map/while/body/eval_jaxpr/hb,qkb->hqk/dot_general | solution.py:352
  63.6 28.5 %fusion.3 = f32[561,561,3]{0,2,1:T(4,128)S(1)} fusion(s32[561,561]{0,1:T(8,128)S(1)} %get-tuple-element.114, f32[3,64]{1,0:T(4,128)S(1)} %copy-done.47), kind=kOutput, calls=%fused_computation.5 | convolution fusion | flops 745259328 | bytes 5036304 | tf_op jit(solution)/shard_map/while/body/eval_jaxpr/hb,qkb->hqk/dot_general | solution.py:352
  92.1 14.3 %fusion.9 = f32[561,561,3]{0,2,1:T(4,128)S(1)} fusion(s32[561,561]{0,1:T(8,128)S(1)} %convert_add_fusion.2, f32[3,32]{1,0:T(4,128)S(1)} %copy-done.48), kind=kOutput, calls=%fused_computation.12 | convolution fusion | flops 372629664 | bytes 5035920 | tf_op jit(solution)/shard_map/while/body/eval_jaxpr/hb,qkb->hqk/dot_general | solution.py:352
  106.4 2.3 fusion.130
  110.9 1.6 fusion.107
  112.5 1.1 copy.76
  113.6 1.3 pad.11.tok_ref
  115.8 1.3 pad.12.cot_ref
  118.7 137.7 %shard_map.374 = (f32[576,768]{1,0:T(8,128)}, f32[576,768]{1,0:T(8,128)}, f32[768,768]{1,0:T(8,128)}, f32[768,768]{1,0:T(8,128)}, f32[8,768]{1,0:T(8,128)}) custom-call(f32[576,768]{1,0:T(8,128)} %pad.11.tok_ref, f32[576,768]{1,0:T(8,128)} %pad.12.cot_ref, bf16[576,192]{1,0:T(8,128)(2,1)} %pad.13.att_ref, f32[192,768]{1,0:T(8,128)} %w_out_ref.1, ...), custom_call_target="tpu_custom_call" | custom-call | flops 4076863488 | bytes 20971520 | tf_op jit(solution)/shard_map/pallas_call | solution.py:307
  256.4 2.0 convolution_convert_fusion
  259.4 1.0 multiply_reduce_fusion
  265.0 1.7 add_add_fusion
  267.6 1.2 convolution_bitcast_fusion
  268.8 2.3 convolution_bitcast_fusion.1
  271.1 1.2 convolution_bitcast_fusion.2
  272.4 1.2 fusion.117
  274.4 2.9 slice.39
  277.3 7.8 %fusion.108 = f32[3,32]{1,0:T(4,128)S(1)} fusion(s32[561,561]{0,1:T(8,128)S(1)} %copy-done.22, bf16[3,561,561]{1,2,0:T(8,128)(2,1)S(1)} %multiply_convert_fusion), kind=kOutput, calls=%fused_computation.137 | convolution fusion | flops 70497504 | bytes 3147594 | tf_op jit(solution)/shard_map/while/body/eval_jaxpr/hqk,qkb->hb/dot_general | solution.py:368
  285.1 14.6 %fusion.111 = f32[3,64]{1,0:T(4,128)S(1)} fusion(s32[561,561]{0,1:T(8,128)S(1)} %copy-done.26, bf16[3,561,561]{1,2,0:T(8,128)(2,1)S(1)} %multiply_convert_fusion), kind=kOutput, calls=%fused_computation.138 | convolution fusion | flops 140995008 | bytes 3147978 | tf_op jit(solution)/shard_map/while/body/eval_jaxpr/hqk,qkb->hb/dot_general | solution.py:368
  299.8 14.9 %fusion.114 = f32[3,64]{1,0:T(4,128)S(1)} fusion(s32[561,561]{0,1:T(8,128)S(1)} %copy-done.24, bf16[3,561,561]{1,2,0:T(8,128)(2,1)S(1)} %multiply_convert_fusion), kind=kOutput, calls=%fused_computation.139 | convolution fusion | flops 140995008 | bytes 3147978 | tf_op jit(solution)/shard_map/while/body/eval_jaxpr/hqk,qkb->hb/dot_general | solution.py:368
  314.7 24.9 %all-reduce.3 = (f32[192]{0:T(256)}, f32[192]{0:T(256)}, f32[768]{0:T(1024)}, f32[768]{0:T(1024)}, f32[768]{0:T(1024)}, /*index=5*/f32[768]{0:T(1024)}, f32[768]...) all-reduce(f32[192]{0:T(256)S(1)} %reduce_sum.65, ...), channel_id=1, replica_groups=mesh['wide'=8,'narrow'=4] {'wide'}, use_global_device_ids=true, to_apply=%region_7.8 | all-reduce | flops 6240 | bytes 49920 | tf_op jit(solution)/shard_map/psum | solution.py:561
  339.6 1.5 all-reduce.8.cloned.1.call-done
  341.1 3.4 slice_add_fusion
  344.5 114.8 %all-reduce.10.cloned.1.call-done = (f32[768,192]{0,1:T(8,128)}, f32[768,192]{0,1:T(8,128)}, f32[768,192]{0,1:T(8,128)}, f32[192,768]{1,0:T(8,128)}, f32[768,768]{1,0:T(8,128)}, /*index=5*/f32[768,768]{1,0:T(8,128)}) async-done(((f32[768,192]{0,1:T(8,128)}, f32[768,192]{0,1:T(8,128)}, f32[768,192]{0,1:T(8,128)}, f32[192,768]{1,0:T(8,128)}, f32[768,768]{1,0:T(8,128)}, /*index=5*/f32[768,768]{1,0:T(8,128)}), ...) | async-done | bytes 7077904 | tf_op jit(solution)/shard_map/psum | solution.py:561
  459.3 2.0 copy.118
  463.8 1.4 copy.122
  465.2 1.1 copy-done.9
  466.3 1.4 copy.123
  (134 shorter events, 15.1 us)
Async XLA Ops:
  7.2 28.3 %copy-start = (f32[3,64]{1,0:T(4,128)S(1)}, f32[3,64]{1,0:T(4,128)}, u32[]{:S(2)}) copy-start(f32[3,64]{1,0:T(4,128)} %param.44) | copy-start | bytes 2308
  7.2 15.2 %copy-start.37 = (s32[561]{0:T(1024)S(1)}, s32[561]{0:T(1024)}, u32[]{:S(2)}) copy-start(s32[561]{0:T(1024)} %param.25) | copy-start | bytes 6736
  7.2 17.7 %copy-start.7 = (f32[768,192]{0,1:T(8,128)S(1)}, f32[768,192]{0,1:T(8,128)}, u32[]{:S(2)}) copy-start(f32[768,192]{0,1:T(8,128)} %param.29) | copy-start | bytes 1769476
  7.2 333.8 %all-reduce.8.cloned.1.call-start = ((), (), s32[]{:S(2)}) async-start(), calls=%async_computation | async-start | bytes 3489792 | tf_op jit(solution)/shard_map/psum | solution.py:541
  22.4 3.0 copy-start.11
  22.4 3.0 copy-start.45
  24.9 67.2 %copy-start.21 = (s32[561,561]{0,1:T(8,128)}, s32[561,561]{0,1:T(8,128)S(1)}, u32[]{:S(2)}) copy-start(s32[561,561]{0,1:T(8,128)S(1)} %convert_add_fusion.2) | copy-start | bytes 3776656
  25.4 81.0 %copy-start.13 = (bf16[561,192]{0,1:T(8,128)(2,1)}, bf16[561,192]{0,1:T(8,128)(2,1)S(1)}, u32[]{:S(2)}) copy-start(bf16[561,192]{0,1:T(8,128)(2,1)S(1)} %convolution_convert_fusion.1) | copy-start | bytes 646276
  35.5 28.1 %copy-start.23 = (s32[561,561]{0,1:T(8,128)}, s32[561,561]{0,1:T(8,128)S(1)}, u32[]{:S(2)}) copy-start(s32[561,561]{0,1:T(8,128)S(1)} %get-tuple-element.113) | copy-start | bytes 3776656
  35.5 28.1 %copy-start.25 = (s32[561,561]{0,1:T(8,128)}, s32[561,561]{0,1:T(8,128)S(1)}, u32[]{:S(2)}) copy-start(s32[561,561]{0,1:T(8,128)S(1)} %get-tuple-element.114) | copy-start | bytes 3776656
  35.5 28.1 %copy-start.47 = (f32[3,64]{1,0:T(4,128)S(1)}, f32[3,64]{1,0:T(4,128)}, u32[]{:S(2)}) copy-start(f32[3,64]{1,0:T(4,128)} %param.43) | copy-start | bytes 2308
  63.6 28.5 %copy-start.48 = (f32[3,32]{1,0:T(4,128)S(1)}, f32[3,32]{1,0:T(4,128)}, u32[]{:S(2)}) copy-start(f32[3,32]{1,0:T(4,128)} %param.42) | copy-start | bytes 1156
  108.8 2.1 copy-start.2
  110.9 2.7 copy-start.4
  113.6 2.1 copy-start.20
  118.0 140.4 %slice-start = ((s8[4362240]{0:T(1024)(128)(4,1)}), s8[167936]{0:T(1024)(128)(4,1)S(1)}, s32[]{:S(2)}) async-start(s8[4362240]{0:T(1024)(128)(4,1)} %bitcast.72), calls=%async_computation.2 | async-start | bytes 335872
  118.7 137.7 %copy-start.30 = (f32[192,768]{1,0:T(8,128)S(1)}, f32[192,768]{1,0:T(8,128)}, u32[]{:S(2)}) copy-start(f32[192,768]{1,0:T(8,128)} %w_out_ref.1) | copy-start | bytes 1769476
  118.7 139.7 %slice-start.1 = ((s8[4362240]{0:T(1024)(128)(4,1)}), s8[4194304]{0:T(1024)(128)(4,1)S(1)}, s32[]{:S(2)}) async-start(s8[4362240]{0:T(1024)(128)(4,1)} %bitcast.72), calls=%async_computation.3 | async-start | bytes 8388608
  259.4 5.2 %copy-start.15 = (bf16[3,64,561]{2,1,0:T(8,128)(2,1)}, bf16[3,64,561]{2,1,0:T(8,128)(2,1)S(1)}, u32[]{:S(2)}) copy-start(bf16[3,64,561]{2,1,0:T(8,128)(2,1)S(1)} %get-tuple-element.112) | copy-start | bytes 646276
  266.7 192.6 %all-reduce.10.cloned.1.call-start = ((), (), s32[]{:S(2)}) async-start(), calls=%async_computation.1 | async-start | bytes 14155776 | tf_op jit(solution)/shard_map/psum | solution.py:561
  267.6 3.5 copy-start.19
  268.8 3.5 copy-start.3
  268.8 3.5 copy-start.27
  274.4 2.9 copy-start.22
  277.3 7.8 %copy-start.26 = (s32[561,561]{0,1:T(8,128)S(1)}, s32[561,561]{0,1:T(8,128)}, u32[]{:S(2)}) copy-start(s32[561,561]{0,1:T(8,128)} %copy-done.25) | copy-start | bytes 3776656
  285.1 14.6 %copy-start.24 = (s32[561,561]{0,1:T(8,128)S(1)}, s32[561,561]{0,1:T(8,128)}, u32[]{:S(2)}) copy-start(s32[561,561]{0,1:T(8,128)} %copy-done.23) | copy-start | bytes 3776656
  459.3 2.1 copy-start.33
  459.3 2.9 copy-start.32
  459.3 3.7 copy-start.31
  461.3 2.5 copy-start.10
  463.8 2.5 copy-start.9
  463.8 3.9 copy-start.1
  (21 other events, 28.4 us)
Sparse Core Ops, SparseCore 0:
  266.8 74.2 all-reduce.7
  346.3 112.9 all-reduce.9

commit v3 on v2

v3 whole, which is shorter than its diff:
```python
import functools
import math

import jax
import jax.numpy as jnp
import numpy as np
from jax import lax
from jax.experimental import pallas as pl
from jax.experimental.pallas import tpu as pltpu
from jax.sharding import PartitionSpec as P

HEAD_DIM = 64
BINS1 = 32
BINS2 = 64
MAX_ORDER = 128
MAX_LAYOUT = 256
PAGE = 561


HIGHEST = lax.Precision.HIGHEST
EPSILON = 1e-05
SCORE_SCALE = 0.125

def bucket_steps(bins, reach):
    halfway = bins // 2
    exact = halfway // 2
    steps = []
    for level in range(1, halfway):
        if level < exact:
            steps.append(level)
        else:
            found = reach + 1
            for count in range(exact, reach + 2):
                value = exact + int(
                    math.log(count / exact) / math.log(reach / exact) * (halfway - exact)
                )
                if min(value, halfway - 1) >= level:
                    found = count
                    break
            steps.append(found)
    return steps


MESH = pl.DeviceIdType.MESH
CH = 96
PC = 48


def erf_of(x):
    x = jnp.clip(x, -3.832506856900711, 3.832506856900711)
    s = x * x
    top = -2.72614225801306e-10
    for term in (2.77068142495902e-08, -2.10102402082508e-06, -5.69250639462346e-05,
                 -7.34990630326855e-04, -2.95459980854025e-03, -1.60960333262415e-02):
        top = top * s + term
    low = -1.45660718464996e-05
    for term in (-2.13374055278905e-04, -1.68282697438203e-03, -7.37332916720468e-03,
                 -1.42647390514189e-02):
        low = low * s + term
    return x * top / low


def normal_cdf(x):
    return 0.5 + 0.5 * erf_of(x * math.sqrt(0.5))


def centre(values):
    c = values - jnp.mean(values, axis=-1, keepdims=True)
    r = lax.rsqrt(jnp.mean(c * c, axis=-1, keepdims=True) + EPSILON)
    return c * r, r


def norm_back(g, n, r, gain):
    m = g * gain
    return r * (m - jnp.mean(m, axis=-1, keepdims=True) - n * jnp.mean(m * n, axis=-1, keepdims=True))


def dot_nn(a, b):
    return lax.dot_general(a, b, (((1,), (0,)), ((), ())), preferred_element_type=jnp.float32)


def dot_nt(a, b):
    return lax.dot_general(a, b, (((1,), (1,)), ((), ())), preferred_element_type=jnp.float32)


def dot_tn(a, b):
    return lax.dot_general(a, b, (((0,), (0,)), ((), ())), preferred_element_type=jnp.float32)


class LineSum:
    def __init__(self, part, rx_in, rx_mid, tot, s_in, s_mid, r_in, r_mid):
        self.part, self.rx_in, self.rx_mid, self.tot = part, rx_in, rx_mid, tot
        self.s_in, self.s_mid, self.r_in, self.r_mid = s_in, s_mid, r_in, r_mid
        w, n = lax.axis_index("wide"), lax.axis_index("narrow")
        self.end = (n == 0) | (n == 3)
        self.mid = jnp.logical_not(self.end)
        self.side = (w, n + 1 - 2 * lax.rem(n, 2))
        self.across = (w, 3 - n)
        self.pieces = part.shape[0] // PC

    def rows(self, p):
        return pl.ds(p * PC, PC) if isinstance(p, int) else pl.ds(pl.multiple_of(p * PC, PC), PC)

    def copy_a(self, p):
        return pltpu.make_async_remote_copy(self.part.at[self.rows(p)], self.rx_in.at[self.rows(p)],
            self.s_in.at[p], self.r_in.at[p], device_id=self.side, device_id_type=MESH)

    def copy_b(self, p):
        return pltpu.make_async_remote_copy(self.part.at[self.rows(p)], self.rx_mid.at[self.rows(p)],
            self.s_mid.at[p], self.r_mid.at[p], device_id=self.across, device_id_type=MESH)

    def copy_t(self, p):
        return pltpu.make_async_remote_copy(self.tot.at[self.rows(p)], self.tot.at[self.rows(p)],
            self.s_in.at[p], self.r_in.at[p], device_id=self.side, device_id_type=MESH)

    def barrier(self, others=0):
        bar = pltpu.get_barrier_semaphore()
        pl.semaphore_signal(bar, inc=1, device_id=self.side, device_id_type=MESH)

        @pl.when(self.mid)
        def _():
            pl.semaphore_signal(bar, inc=1, device_id=self.across, device_id_type=MESH)

        @pl.when(self.end)
        def _():
            pl.semaphore_wait(bar, 1 + others)

        @pl.when(self.mid)
        def _():
            pl.semaphore_wait(bar, 2 + others)

    def free_part(self, p):
        @pl.when(self.end)
        def _():
            self.copy_a(p).wait_send()

        @pl.when(self.mid)
        def _():
            self.copy_b(p).wait_send()

    def finish(self, p, first):
        self.copy_b(p).wait_recv()
        if not first:
            self.copy_t(p).wait_send()
        self.tot[self.rows(p), :] = self.part[self.rows(p), :] + self.rx_mid[self.rows(p), :]
        self.copy_t(p).start()

    def slot(self, p, order):
        @pl.when(self.end)
        def _():
            self.copy_a(p).start()

        @pl.when(self.mid)
        def _():
            self.copy_a(p).wait_recv()
            self.part[self.rows(p), :] += self.rx_in[self.rows(p), :]
            self.copy_b(p).start()

            @pl.when(p > 0)
            def _():
                self.finish(p - 1, order == 0)

            if order > 0:
                @pl.when(p == 0)
                def _():
                    self.finish(self.pieces - 1, order == 1)

    def send_end(self, p):
        @pl.when(self.end)
        def _():
            self.copy_a(p).start()

    def slot_mid(self, p):
        @pl.when(self.mid)
        def _():
            self.copy_a(p).wait_recv()
            self.part[self.rows(p), :] += self.rx_in[self.rows(p), :]
            self.copy_b(p).start()
            if p > 0:
                self.finish(p - 1, True)

    def last(self, first):
        @pl.when(self.mid)
        def _():
            self.finish(self.pieces - 1, first)

    def want(self, p):
        @pl.when(self.end)
        def _():
            self.copy_t(p).wait_recv()

    def drain(self):
        def one(p, c):
            self.free_part(p)

            @pl.when(self.mid)
            def _():
                self.copy_t(p).wait_send()
            return c
        lax.fori_loop(0, self.pieces, one, 0)


def middle_kernel(tok_ref, cot_ref, att_ref, w_out_ref, w_in_ref, w_down_ref, bo_r, g1_r, b1_r, bi_r, bd_r, g2_r, b2_r, perm,
                  out_ref, gres_ref, dwin_ref, dwdown_ref, small_ref,
                  part, rx_in, rx_mid, tot, res, hid, pre, act, gff, hlow, gpre, wo, wi, wd, outp, vec_s,
                  s_in, s_mid, r_in, r_mid):
    line = LineSum(part, rx_in, rx_mid, tot, s_in, s_mid, r_in, r_mid)
    steps = part.shape[0] // CH
    k = CH // PC
    for i, vector in enumerate((bo_r, g1_r, b1_r, bi_r, bd_r, g2_r, b2_r)):
        vec_s[i, :] = vector[...]
    b_out, g1, b1, b_in, b_down, g2, b2 = (vec_s[i:i + 1, :] for i in range(7))
    wo[...] = jnp.zeros_like(wo)
    wo[0:w_out_ref.shape[0], :] = w_out_ref[...].astype(jnp.bfloat16)
    line.barrier()

    def rows(c):
        return pl.ds(pl.multiple_of(c * CH, CH), CH)

    def branch_step(c, carry):
        r = rows(c)
        part[r, :] = dot_nn(att_ref[r, :], wo[...])
        for j in range(k):
            line.slot(c * k + j, 0)
        return carry
    lax.fori_loop(0, steps, branch_step, 0)
    wi[...] = w_in_ref[...].astype(jnp.bfloat16)
    wd[...] = w_down_ref[...].astype(jnp.bfloat16)
    small_ref[...] = jnp.zeros_like(small_ref)
    outp[...] = jnp.zeros_like(outp)

    def open_step(c):
        for j in range(k):
            line.want(c * k + j)
        for j in range(k):
            line.free_part(c * k + j)

    def forward_step(c, carry):
        r = rows(c)
        open_step(c)
        one = tok_ref[r, :] + (tot[r, :] + b_out)
        res[r, :] = one
        n, _ = centre(one)
        hidden = n * g1 + b1
        hid[r, :] = hidden
        low = hidden.astype(jnp.bfloat16)
        hlow[r, :] = low
        u = dot_nn(low, wi[...]) + b_in
        pre[r, :] = u
        a = (u * normal_cdf(u)).astype(jnp.bfloat16)
        act[r, :] = a
        part[r, :] = dot_nn(a, wd[...])
        for j in range(k):
            line.slot(c * k + j, 1)
        return carry
    lax.fori_loop(0, steps, forward_step, 0)

    def add_row(i, rows_value):
        small_ref[i:i + 1, :] += jnp.sum(rows_value, axis=0, keepdims=True)

    def back_step(c, carry):
        r = rows(c)
        open_step(c)
        two = hid[r, :] + (tot[r, :] + b_down)
        n, rs = centre(two)
        g = cot_ref[r, :]
        add_row(0, g * n)
        add_row(1, g)
        back = norm_back(g, n, rs, g2)
        hid[r, :] = back
        low = back.astype(jnp.bfloat16)
        gff[r, :] = low
        add_row(2, low.astype(jnp.float32))
        ga = dot_nt(low, wd[...])
        u = pre[r, :]
        slope = normal_cdf(u) + u * (jnp.exp(-0.5 * u * u) * (1.0 / math.sqrt(2.0 * math.pi)))
        gp = (ga * slope).astype(jnp.bfloat16)
        gpre[r, :] = gp
        add_row(3, gp.astype(jnp.float32))
        part[r, :] = dot_nt(gp, wi[...])
        for j in range(k):
            line.slot(c * k + j, 2)
        total = outp[...]
        for piece in split3(n * g2 + b2):
            total = total + dot_tn(perm[r, :], piece)
        outp[...] = total
        return carry
    lax.fori_loop(0, steps, back_step, 0)
    line.last(False)
    dwdown_ref[...] = dot_tn(act[...], gff[...])
    dwin_ref[...] = dot_tn(hlow[...], gpre[...])

    def close_step(c, carry):
        r = rows(c)
        for j in range(k):
            line.want(c * k + j)
        g = hid[r, :] + tot[r, :]
        n, rs = centre(res[r, :])
        add_row(4, g * n)
        add_row(5, g)
        back = norm_back(g, n, rs, g1)
        gres_ref[r, :] = back
        add_row(6, back.astype(jnp.bfloat16).astype(jnp.float32))
        return carry
    lax.fori_loop(0, steps, close_step, 0)
    out_ref[...] = outp[0:out_ref.shape[0], :]
    line.drain()


def middle(tok, cot, att, w_out, w_in, w_down, b_out, g1, b1, b_in, b_down, g2, b2, perm):
    rows, d = tok.shape
    f = w_in.shape[1]
    pieces = rows // PC
    f32, bf = jnp.float32, jnp.bfloat16
    shapes = (jax.ShapeDtypeStruct((PAGE, d), f32), jax.ShapeDtypeStruct((rows, d), f32),
              jax.ShapeDtypeStruct((d, f), f32), jax.ShapeDtypeStruct((f, d), f32),
              jax.ShapeDtypeStruct((8, d), f32))
    vm = pl.BlockSpec(memory_space=pltpu.VMEM)
    big = [pltpu.VMEM((rows, d), f32) for _ in range(6)]
    return pl.pallas_call(
        middle_kernel, out_shape=shapes, in_specs=[vm] * 14, out_specs=[vm] * 5,
        scratch_shapes=big + [pltpu.VMEM((rows, f), f32), pltpu.VMEM((rows, f), bf), pltpu.VMEM((rows, d), bf),
                              pltpu.VMEM((rows, d), bf), pltpu.VMEM((rows, f), bf),
                              pltpu.VMEM((256, d), bf), pltpu.VMEM((d, f), bf), pltpu.VMEM((f, d), bf),
                              pltpu.VMEM((WIDE_ROWS, d), f32), pltpu.VMEM((8, d), f32)]
        + [pltpu.SemaphoreType.DMA((pieces,))] * 4,
        compiler_params=pltpu.CompilerParams(collective_id=0, has_side_effects=True, vmem_limit_bytes=56 << 20),
        cost_estimate=pl.CostEstimate(flops=6 * 2 * rows * d * f, bytes_accessed=20 << 20, transcendentals=rows * f),
    )(tok, cot, att, w_out, w_in, w_down, b_out, g1, b1, b_in, b_down, g2, b2, perm)


WIDE_ROWS = 640
ROWS = 576


def bucket_number(offset, bins, reach):
    halfway = bins // 2
    steps = bucket_steps(bins, reach)
    return (halfway if offset > 0 else 0) + sum(1 for s in steps if abs(offset) >= s)


def choose_matrix(offsets, bins, reach):
    out = np.zeros((bins, len(offsets)), np.float32)
    for place, offset in enumerate(offsets):
        out[bucket_number(offset, bins, reach), place] = 1.0
    return out


def split3(x):
    hi = x.astype(jnp.bfloat16)
    rest = x - hi.astype(jnp.float32)
    mid = rest.astype(jnp.bfloat16)
    return hi, mid, (rest - mid.astype(jnp.float32)).astype(jnp.bfloat16)


def split2(x):
    hi = x.astype(jnp.bfloat16)
    return hi, (x - hi.astype(jnp.float32)).astype(jnp.bfloat16)


def exact_dot(a, b, dims):
    return lax.dot_general(a, b, (dims, ((), ())), precision=HIGHEST, preferred_element_type=jnp.float32)


def lanes_of(h, shape):
    lane = lax.broadcasted_iota(jnp.int32, shape, 1)
    return (lane >= h * HEAD_DIM) & (lane < (h + 1) * HEAD_DIM)


def row_blocks(body):
    full = ROWS // 128

    def step(m, carry):
        body(m, 128)
        return carry
    lax.fori_loop(0, full, step, 0)
    if ROWS % 128:
        body(full, ROWS % 128)


def block_rows(m, n):
    return pl.ds(pl.multiple_of(m * 128, 128), n)


def block_window(m):
    return pl.ds(pl.multiple_of(512 - m * 128, 128), WIDE_ROWS)


def head_kernel(tok, cot, reg, rank, box, wq, wk, wv, bq, bv, to, tx, ty, so, sxy,
                tokp, cotp, low, perm, q_ref, k_ref, v_ref, prob, att, ob, obf, ws,
                rows_s, vec_s, split_s, base, amat, ob4, att_f):
    f32, bf = jnp.float32, jnp.bfloat16
    n = PAGE
    rows_s[...] = jnp.full(rows_s.shape, 1e4, f32)
    rows_s[0, 0:n] = reg[...].astype(f32)
    rows_s[1, 0:n] = rank[...].astype(f32)
    rows_s[2:4, 0:n] = box[...].astype(f32)
    region_row, rank_row = rows_s[0:1, :], rows_s[1:2, :]
    i0 = lax.broadcasted_iota(jnp.int32, (WIDE_ROWS, WIDE_ROWS), 0)
    i1 = lax.broadcasted_iota(jnp.int32, (WIDE_ROWS, WIDE_ROWS), 1)
    region_col = jnp.sum(jnp.where(i0 == i1, region_row, 0.0), axis=1, keepdims=True)
    place = jnp.sum(jnp.where(region_col < region_row, 1.0, 0.0), axis=0, keepdims=True) + rank_row
    perm[...] = jnp.where(i0.astype(f32) == place, 1.0, 0.0).astype(bf)
    split_s[...] = jnp.zeros_like(split_s)

    def sort_rows(source, target, first):
        parts = split3(source[...])
        for i in range(3):
            split_s[i, 0:n, :] = parts[i]
        y = dot_nn(perm[...], split_s[0])
        if first is not None:
            first[...] = y.astype(bf)
        target[...] = y[0:ROWS, :]
        for i in range(1, 3):
            target[...] += dot_nn(perm[0:ROWS, :], split_s[i])
    sort_rows(tok, tokp, low)
    code = lax.broadcasted_iota(jnp.int32, (128, WIDE_ROWS), 0).astype(f32)
    for i in range(2):
        row = rows_s[2 + i:3 + i, :]
        one = dot_nt(perm[...], jnp.where(code == row, 1.0, 0.0).astype(bf)).astype(bf)
        ob[:, 128 * i:128 * (i + 1)] = one
        ob4[:, 256 * i:256 * i + 128] = one
        ob4[:, 256 * i + 128:256 * i + 256] = one
        obf[:, 128 * i:128 * (i + 1)] = dot_nt(perm[...], jnp.where(127.0 - code == row, 1.0, 0.0).astype(bf)).astype(bf)
    width = wq.shape[0]
    ws[...] = jnp.zeros_like(ws)
    for i, weight in enumerate((wq, wk, wv)):
        ws[i, 0:width, :] = weight[...].astype(bf)
    vec_s[...] = jnp.zeros_like(vec_s)
    vec_s[0, 0:width] = bq[...]
    vec_s[1, 0:width] = bv[...]
    q_ref[...] = ((dot_nt(low[...], ws[0]) + vec_s[0:1, :]).astype(bf) * SCORE_SCALE).astype(bf)
    k_ref[...] = dot_nt(low[...], ws[1]).astype(bf)
    v_ref[...] = (dot_nt(low[...], ws[2]) + vec_s[1:2, :]).astype(bf)
    row_o = exact_dot(to[...], so[...], ((1,), (0,)))
    row_xy = (exact_dot(tx[...], sxy[...], ((1,), (0,))), exact_dot(ty[...], sxy[...], ((1,), (0,))))
    heads = to.shape[0]
    for h in range(heads):
        base[...] = pltpu.roll(jnp.broadcast_to(row_o[h:h + 1, :], base.shape), 0, 1, stride=1, stride_axis=0)
        for i in range(2):
            table = pltpu.roll(jnp.broadcast_to(row_xy[i][h:h + 1, :], (128, 256)), 0, 1, stride=1, stride_axis=0)
            pair = jnp.concatenate(split2(table[:, 0:128]), axis=1)
            amat[:, 256 * i:256 * (i + 1)] = dot_nn(ob[:, 128 * i:128 * (i + 1)], pair).astype(bf)

        def block(m, rows, h=h):
            r = block_rows(m, rows)
            qh = jnp.where(lanes_of(h, (rows, 256)), q_ref[r, :], jnp.zeros((), bf))
            s = dot_nt(qh, k_ref[...]) + dot_nt(amat[r, :], ob4[...]) + base[0:rows, block_window(m)]
            s = jnp.where(lax.broadcasted_iota(jnp.int32, s.shape, 1) < n, s, -1e30)
            e = jnp.exp(s - jnp.max(s, axis=1, keepdims=True))
            p = e / jnp.sum(e, axis=1, keepdims=True)
            prob[h, r, :] = p
            pv = dot_nn(p.astype(bf), v_ref[...])
            if h > 0:
                pv = jnp.where(lanes_of(h, (rows, 256)), pv, att_f[r, :])
            att_f[r, :] = pv
        row_blocks(block)
    att[...] = jnp.zeros_like(att)
    att[0:ROWS, :] = att_f[...].astype(bf)
    sort_rows(cot, cotp, None)


def head(tok, cot, reg, rank, box, wq, wk, wv, bq, bv, to, tx, ty, so, sxy):
    f32, bf = jnp.float32, jnp.bfloat16
    d = tok.shape[1]
    heads = to.shape[0]
    sd = jax.ShapeDtypeStruct
    W, R = WIDE_ROWS, ROWS
    shapes = (sd((R, d), f32), sd((R, d), f32), sd((W, d), bf), sd((W, W), bf), sd((W, 256), bf), sd((W, 256), bf),
              sd((W, 256), bf), sd((heads, R, W), f32), sd((W, 256), bf), sd((W, 256), bf), sd((W, 256), bf), sd((3, 256, d), bf))
    vm = pl.BlockSpec(memory_space=pltpu.VMEM)
    return pl.pallas_call(
        head_kernel, out_shape=shapes, in_specs=[vm] * 15, out_specs=[vm] * 12,
        scratch_shapes=[pltpu.VMEM((8, W), f32), pltpu.VMEM((8, 256), f32),
                        pltpu.VMEM((3, W, d), bf), pltpu.VMEM((128, 1280), f32), pltpu.VMEM((W, 512), bf),
                        pltpu.VMEM((W, 512), bf), pltpu.VMEM((R, 256), f32)],
        compiler_params=pltpu.CompilerParams(vmem_limit_bytes=56 << 20),
        cost_estimate=pl.CostEstimate(flops=10 ** 10, bytes_accessed=20 << 20, transcendentals=heads * R * W),
    )(tok, cot, reg, rank, box, wq, wk, wv, bq, bv, to, tx, ty, so, sxy)


class CubeSum:
    def __init__(self, ref, rx1, rx2, rx3, rx4, rxb, ssem, rsem, free, bits):
        self.ref, self.rx1, self.rx2, self.rx3, self.rx4, self.rxb = ref, rx1, rx2, rx3, rx4, rxb
        self.ssem, self.rsem, self.free = ssem, rsem, free
        w, n = lax.axis_index("wide"), lax.axis_index("narrow")
        self.bit = [lax.rem(lax.div(w, 2 ** i), 2) for i in range(bits)]
        self.to = [(w + 2 ** i * (1 - 2 * self.bit[i]), n) for i in range(bits)]
        self.rows = ref.shape[0]
        half = self.rows // 2
        self.half, self.stream, self.eighth, self.piece = half, half // 2, half // 4, half // 8
        self.own = self.bit[0] * half
        self.axes = ((1, 2), (2, 1))
        self.extra = range(3, bits)

    def at(self, start, size):
        return pl.ds(pl.multiple_of(start, self.piece), size)

    def base1(self, s, other):
        b = self.bit[self.axes[s][0]]
        b = 1 - b if other else b
        return self.own + s * self.stream + b * self.eighth

    def base2(self, s, other):
        b = self.bit[self.axes[s][1]]
        b = 1 - b if other else b
        return self.base1(s, False) + b * self.piece

    def copy(self, src, dst, i, axis):
        return pltpu.make_async_remote_copy(src, dst, self.ssem.at[i], self.rsem.at[i], device_id=self.to[axis],
                                            device_id_type=MESH)

    def core_out(self):
        return self.copy(self.ref.at[self.at((1 - self.bit[0]) * self.half, self.half)], self.rx1, 0, 0)

    def first(self, s):
        return self.copy(self.ref.at[self.at(self.base1(s, True), self.eighth)], self.rx2.at[s], 1 + s, self.axes[s][0])

    def second(self, s):
        return self.copy(self.ref.at[self.at(self.base2(s, True), self.piece)], self.rx3.at[s], 3 + s, self.axes[s][1])

    def back2(self, s):
        r = self.at(self.base2(s, False), self.piece)
        return self.copy(self.ref.at[r], self.rxb.at[s], 5 + s, self.axes[s][1])

    def back1(self, s):
        r = self.at(self.base1(s, False), self.eighth)
        return self.copy(self.ref.at[r], self.ref.at[r], 7 + s, self.axes[s][0])

    def core_back(self):
        r = self.at(self.own, self.half)
        return self.copy(self.ref.at[r], self.ref.at[r], 9, 0)

    def more(self, e, s):
        i = e - 3
        return self.copy(self.ref.at[self.at(self.base2(s, False), self.piece)], self.rx4.at[i, s], 10 + 2 * i + s, e)

    def release(self, i, axis):
        pl.semaphore_signal(self.free.at[i], inc=1, device_id=self.to[axis], device_id_type=MESH)

    def step(self, i):
        if i == 0:
            self.core_out().start()
        if i == 1:
            self.core_out().wait_recv()
            self.ref[self.at(self.own, self.half), :] += self.rx1[...]
            for s in range(2):
                self.first(s).start()
            self.core_out().wait_send()
            self.release(0, 0)
        if i == 2:
            for s in range(2):
                self.first(s).wait()
                self.release(1 + s, self.axes[s][0])
                self.ref[self.at(self.base1(s, False), self.eighth), :] += self.rx2[s]
                self.second(s).start()
        if i == 3:
            for s in range(2):
                self.second(s).wait()
                self.ref[self.at(self.base2(s, False), self.piece), :] += self.rx3[s]
            for e in self.extra:
                for s in range(2):
                    self.more(e, s).start()
                for s in range(2):
                    self.more(e, s).wait()
                    self.ref[self.at(self.base2(s, False), self.piece), :] += self.rx4[e - 3, s]
            for s in range(2):
                self.back2(s).start()
        if i == 4:
            for s in range(2):
                self.back2(s).wait_recv()
                self.ref[self.at(self.base2(s, True), self.piece), :] = self.rxb[s]
                pl.semaphore_wait(self.free.at[1 + s], 1)
                self.back1(s).start()
        if i == 5:
            for s in range(2):
                self.back1(s).wait_recv()
            pl.semaphore_wait(self.free.at[0], 1)
            self.core_back().start()
        if i == 6:
            self.core_back().wait()
            for s in range(2):
                self.back2(s).wait_send()
                self.back1(s).wait_send()


def tail_kernel(bits, gres, small_in, dwi_in, dwd_in, wout, att, q_ref, k_ref, v_ref, prob, ob, obf, low, ws, perm, sgo, sgxy,
                gin, gat, gwi, gwd, sm,
                part, rx_in, rx_mid, tot, rx1, rx2, rx3, rx4, rxb, rxs, ds_s, pl_s, ga, gt, qt, dkt, dvt, dqf, dq, dk, dv, acc, wos, ginp,
                s_in, s_mid, r_in, r_mid, cs, cr, cf, ss, sr):
    f32, bf = jnp.float32, jnp.bfloat16
    n = PAGE
    heads = prob.shape[0]
    width = wout.shape[0]
    line = LineSum(part, rx_in, rx_mid, tot, s_in, s_mid, r_in, r_mid)
    cube = [CubeSum(ref, rx1.at[i], rx2.at[i], rx3.at[i], rx4.at[i], rxb.at[i], cs.at[i], cr.at[i], cf.at[i], bits)
            for i, ref in enumerate((gwi, gwd, gat))]
    gwi[...] = dwi_in[...]
    gwd[...] = dwd_in[...]
    bar = pltpu.get_barrier_semaphore()
    for to in cube[0].to:
        pl.semaphore_signal(bar, inc=1, device_id=to, device_id_type=MESH)
    line.barrier(bits)
    cube[0].step(0)
    cube[1].step(0)

    sm[...] = jnp.zeros_like(sm)
    sm[0:8, :] = small_in[...]
    gb = gres[...].astype(bf)
    wos[...] = jnp.zeros_like(wos)
    wos[0:width, :] = wout[...].astype(bf)
    ga[...] = jnp.zeros_like(ga)
    ga[0:ROWS, :] = dot_nt(gb, wos[...]).astype(bf)
    gt[...] = jnp.transpose(ga[...])
    qt[...] = jnp.transpose(q_ref[...])
    ds_s[...] = jnp.zeros_like(ds_s)
    pl_s[...] = jnp.zeros_like(pl_s)
    dkt[...] = jnp.zeros_like(dkt)
    dvt[...] = jnp.zeros_like(dvt)
    dqf[...] = jnp.zeros_like(dqf)
    gat[3 * width:4 * width, :] = dot_tn(att[0:ROWS, :], gb)[0:width, :]
    flip = (lax.broadcasted_iota(jnp.int32, (128, 128), 0) + lax.broadcasted_iota(jnp.int32, (128, 128), 1)) == 127
    flip = jnp.where(flip, 1.0, 0.0).astype(bf)
    for h in range(heads):
        acc[...] = jnp.zeros_like(acc)

        def block(m, rows, h=h):
            r = block_rows(m, rows)
            gh = jnp.where(lanes_of(h, (rows, 256)), ga[r, :], jnp.zeros((), bf))
            dp = dot_nt(gh, v_ref[...])
            p = prob[h, r, :]
            inner = jnp.sum(p * dp, axis=1, keepdims=True)
            ds = (p * (dp - inner)).astype(bf)
            ds_s[r, :] = ds
            pl_s[r, :] = p.astype(bf)
            dqh = dot_nn(ds, k_ref[...])
            dqf[r, :] = jnp.where(lanes_of(h, (rows, 256)), dqh, dqf[r, :])
            acc[0:rows, block_window(m)] += ds.astype(f32)
        row_blocks(block)
        hr = pl.ds(h * HEAD_DIM, HEAD_DIM)
        dkt[hr, :] = dot_nn(qt[hr, :], ds_s[...])
        dvt[hr, :] = dot_nn(gt[hr, :], pl_s[...])
        u = jnp.concatenate(split2(dot_nn(ds_s[...], ob[...])), axis=1)
        g = dot_tn(obf[...], u)
        for i in range(2):
            b = 128 * i
            both = g[b:b + 128, b:b + 128] + g[b:b + 128, 256 + b:384 + b]
            both = jnp.concatenate([both, jnp.zeros_like(both)], axis=1)
            line_sum = jnp.sum(pltpu.roll(both, 0, 1, stride=1, stride_axis=0), axis=0, keepdims=True)
            sm[13 + heads * i + h:14 + heads * i + h, 0:BINS2] = exact_dot(line_sum, sgxy[...], ((1,), (1,)))
        hi, lo = split2(acc[...])
        turned = dot_nn(flip, hi) + dot_nn(flip, lo)
        line_sum = jnp.sum(pltpu.roll(turned, 0, 1, stride=1, stride_axis=0), axis=0, keepdims=True)
        sm[10 + h:11 + h, 0:BINS1] = exact_dot(line_sum, sgo[...], ((1,), (1,)))
        if h == 1:
            cube[0].step(1)
            cube[1].step(1)
    dq[...] = jnp.zeros_like(dq)
    dq[0:ROWS, :] = (dqf[...] * SCORE_SCALE).astype(bf)
    dk[...] = jnp.transpose(dkt[...]).astype(bf)
    dv[...] = jnp.transpose(dvt[...]).astype(bf)
    sm[8:9, 0:256] = jnp.sum(dq[...].astype(f32), axis=0, keepdims=True)
    sm[9:10, 0:256] = jnp.sum(dv[...].astype(f32), axis=0, keepdims=True)
    k = CH // PC
    for c in range(ROWS // CH):
        r = slice(c * CH, (c + 1) * CH)
        part[r, :] = dot_nn(dq[r, :], ws[0]) + dot_nn(dk[r, :], ws[1]) + dot_nn(dv[r, :], ws[2])
        for j in range(k):
            line.send_end(c * k + j)

    bit_to = cube[0].to

    def small_copy(i):
        return pltpu.make_async_remote_copy(sm, rxs.at[i], ss.at[i], sr.at[i], device_id=bit_to[i], device_id_type=MESH)

    def small_step(i):
        if i > 0:
            small_copy(i - 1).wait()
            sm[...] += rxs[i - 1]
        if i < bits:
            small_copy(i).start()

    def weight_grad(i):
        gat[i * width:(i + 1) * width, :] = dot_tn((dq, dk, dv)[i][...], low[...])[0:width, :]

    ginp[...] = jnp.zeros_like(ginp)

    def consume(c):
        for j in range(k):
            line.want(c * k + j)
        r = slice(c * CH, (c + 1) * CH)
        y = gres[r, :] + tot[r, :]
        total = ginp[...]
        for piece in split3(y):
            total = total + dot_tn(perm[r, :], piece)
        ginp[...] = total

    jobs = {0: [(weight_grad, 0)], 1: [(weight_grad, 1)], 2: [(weight_grad, 2), (cube[2].step, 0), (small_step, 0)],
            3: [(cube[0].step, 2), (cube[1].step, 2)], 4: [(cube[2].step, 1), (small_step, 1)],
            5: [(cube[0].step, 3), (cube[1].step, 3)], 6: [(small_step, 2), (consume, 0)],
            7: [(cube[2].step, 2), (cube[0].step, 4), (cube[1].step, 4)], 8: [(small_step, 3), (consume, 1)],
            9: [(cube[2].step, 3)], 10: [(consume, 2)], 11: [(cube[2].step, 4), (cube[0].step, 5), (cube[1].step, 5)]}
    for p in range(line.pieces):
        line.slot_mid(p)
        for job, arg in jobs.get(p, ()):
            job(arg)
    line.last(True)
    for i in range(4, bits + 1):
        small_step(i)
    consume(3)
    consume(4)
    cube[2].step(5)
    consume(5)
    for c in cube:
        c.step(6)
    gin[...] = ginp[0:n, :]
    line.drain()


def tail(bits, gres, small_in, dwi, dwd, wout, att, q, k, v, prob, ob, obf, low, ws, perm, sgo, sgxy):
    f32, bf = jnp.float32, jnp.bfloat16
    d = gres.shape[1]
    f = dwi.shape[1]
    width = wout.shape[0]
    sd = jax.ShapeDtypeStruct
    W, R = WIDE_ROWS, ROWS
    pieces = R // PC
    more = max(bits - 3, 1)
    shapes = (sd((PAGE, d), f32), sd((4 * width, d), f32),
              sd((d, f), f32), sd((f, d), f32), sd((24, d), f32))
    vm = pl.BlockSpec(memory_space=pltpu.VMEM)
    v_ = pltpu.VMEM
    return pl.pallas_call(
        functools.partial(tail_kernel, bits), out_shape=shapes, in_specs=[vm] * 17, out_specs=[vm] * 5,
        scratch_shapes=[v_((R, d), f32)] * 4 + [v_((3, d // 2, d), f32), v_((3, 2, d // 8, d), f32),
                        v_((3, 2, d // 16, d), f32), v_((3, more, 2, d // 16, d), f32), v_((3, 2, d // 16, d), f32), v_((bits, 24, d), f32),
                        v_((W, W), bf), v_((W, W), bf), v_((W, 256), bf), v_((256, W), bf), v_((256, W), bf),
                        v_((256, W), f32), v_((256, W), f32), v_((R, 256), f32), v_((W, 256), bf), v_((W, 256), bf), v_((W, 256), bf),
                        v_((128, 1280), f32), v_((256, d), bf), v_((W, d), f32)]
        + [pltpu.SemaphoreType.DMA((pieces,))] * 4
        + [pltpu.SemaphoreType.DMA((3, 10 + 2 * more))] * 2 + [pltpu.SemaphoreType.REGULAR((3, 3))] + [pltpu.SemaphoreType.DMA((bits,))] * 2,
        compiler_params=pltpu.CompilerParams(collective_id=1, has_side_effects=True, vmem_limit_bytes=60 << 20),
        cost_estimate=pl.CostEstimate(flops=10 ** 10, bytes_accessed=20 << 20, transcendentals=0),
    )(gres, small_in, dwi, dwd, wout, att, q, k, v, prob, ob, obf, low, ws, perm, sgo, sgxy)


def finish_kernel(out_in, gin_in, gat_in, gwi_in, gwd_in, sm, out, gin, gwq, gwk, gwv, gwo, gwi, gwd, *rest):
    vectors, (b_out, b_gin, b_gat, b_gwi, b_gwd, sem_in, sem_out) = rest[:12], rest[12:]
    width = gwo.shape[0]
    heads = vectors[9].shape[0]
    whole = [(out_in, b_out, out), (gin_in, b_gin, gin), (gwi_in, b_gwi, gwi), (gwd_in, b_gwd, gwd)]
    for i, g in enumerate((gwq, gwk, gwv, gwo)):
        r = pl.ds(i * width, width)
        whole.append((gat_in.at[r], b_gat.at[r], g))
    inward = [pltpu.make_async_copy(a, b, sem_in.at[i]) for i, (a, b, _) in enumerate(whole)]
    outward = [pltpu.make_async_copy(b, c, sem_out.at[i]) for i, (_, b, c) in enumerate(whole)]
    for c in inward:
        c.start()
    for i in range(7):
        vectors[i][...] = sm[i, :]
    vectors[7][...] = sm[8, 0:width]
    vectors[8][...] = sm[9, 0:width]
    vectors[9][...] = sm[10:10 + heads, 0:BINS1]
    vectors[10][...] = sm[10 + heads:10 + 2 * heads, 0:BINS2]
    vectors[11][...] = sm[10 + 2 * heads:10 + 3 * heads, 0:BINS2]
    for c, o in zip(inward, outward):
        c.wait()
        o.start()
    for o in outward:
        o.wait()


def finish(heads, width, out, gin, gat, gwi, gwd, sm):
    f32 = jnp.float32
    sd = jax.ShapeDtypeStruct
    d = gat.shape[1]
    like = lambda x: sd(x.shape, f32)
    shapes = (like(out), like(gin)) + (sd((width, d), f32),) * 4 + (like(gwi), like(gwd)) + (sd((d,), f32),) * 7 \
        + (sd((width,), f32),) * 2 + (sd((heads, BINS1), f32), sd((heads, BINS2), f32), sd((heads, BINS2), f32))
    vm, hbm = pl.BlockSpec(memory_space=pltpu.VMEM), pl.BlockSpec(memory_space=pl.ANY)
    return pl.pallas_call(
        finish_kernel, out_shape=shapes, in_specs=[hbm] * 5 + [vm], out_specs=[hbm] * 8 + [vm] * 12,
        scratch_shapes=[pltpu.VMEM(x.shape, f32) for x in (out, gin, gat, gwi, gwd)] + [pltpu.SemaphoreType.DMA((8,))] * 2,
        compiler_params=pltpu.CompilerParams(vmem_limit_bytes=56 << 20),
    )(out, gin, gat, gwi, gwd, sm)


def local(
    bits,
    tokens,
    region,
    order_rank,
    box_coords,
    w_query,
    b_query,
    w_key,
    w_value,
    b_value,
    w_out,
    b_out,
    ln1_gain,
    ln1_bias,
    w_in,
    b_in,
    w_down,
    b_down,
    ln2_gain,
    ln2_bias,
    rel_order,
    rel_x,
    rel_y,
    cotangent,
):
    so = choose_matrix([i - 512 if i < 1152 else i - 1792 for i in range(1280)], BINS1, MAX_ORDER)
    sxy = choose_matrix([i if i < 128 else i - 256 for i in range(256)], BINS2, MAX_LAYOUT)
    sgo = choose_matrix([i - 639 for i in range(1280)], BINS1, MAX_ORDER)
    sgxy = choose_matrix([i - 127 for i in range(256)], BINS2, MAX_LAYOUT)
    width = w_out.shape[0]
    heads = rel_order.shape[0]
    tokp, cotp, low, perm, q, k, v, prob, att, ob, obf, ws = head(
        tokens, cotangent, region, order_rank, box_coords, w_query.T, w_key.T, w_value.T, b_query, b_value, rel_order, rel_x, rel_y, so, sxy)
    output, gres, dwi, dwd, small = middle(
        tokp, cotp, att, w_out, w_in, w_down, b_out, ln1_gain, ln1_bias, b_in, b_down, ln2_gain, ln2_bias, perm)
    gin, gat, gwi, gwd, sm = tail(
        bits, gres, small, dwi, dwd, w_out, att, q, k, v, prob, ob, obf, low, ws, perm, sgo, sgxy)
    (output, gin, gwq, gwk, gwv, gwo, gwi, gwd, l2g, l2b, bd, bi, l1g, l1b, bo, gbq, gbv, ro, rx, ry) = finish(
        heads, width, output, gin, gat, gwi, gwd, sm)
    return (output, gin, gwq.T, gbq, gwk.T, gwv.T, gbv, gwo, bo, l1g, l1b, gwi, bi,
            gwd, bd, l2g, l2b, ro, rx, ry)


def solution(mesh):
    in_specs = (
        P("wide", None),
        P("wide"),
        P("wide"),
        P(None, "wide"),
        P(None, "narrow"),
        P("narrow"),
        P(None, "narrow"),
        P(None, "narrow"),
        P("narrow"),
        P("narrow", None),
        P(),
        P(),
        P(),
        P(None, "narrow"),
        P("narrow"),
        P("narrow", None),
        P(),
        P(),
        P(),
        P("narrow", None),
        P("narrow", None),
        P("narrow", None),
        P("wide", None),
    )
    out_specs = (
        P("wide", None),
        P("wide", None),
        P(None, "narrow"),
        P("narrow"),
        P(None, "narrow"),
        P(None, "narrow"),
        P("narrow"),
        P("narrow", None),
        P(),
        P(),
        P(),
        P(None, "narrow"),
        P("narrow"),
        P("narrow", None),
        P(),
        P(),
        P(),
        P("narrow", None),
        P("narrow", None),
        P("narrow", None),
    )
    bits = mesh.shape["wide"].bit_length() - 1
    return jax.shard_map(functools.partial(local, bits), mesh=mesh, in_specs=in_specs, out_specs=out_specs, check_vma=False)
```

time: 479 us -> 265 us (0.55)
  matrix products: 127 us -> 0 us
  Pallas kernels: 138 us -> 262 us
  waiting for transfers between devices: 116 us -> 0 us
  other arithmetic: 32.1 us -> 0 us
  blocking collectives: 24.9 us -> 0 us
  local copies, waits for them, and re-layouts: 21.4 us -> 0 us
  between operations: 15.2 us -> 0.86 us
    dot_general x23 -> x0, matrix products: 127 us -> none  [the longest x3 70.8 us: relative_one_page(): jnp.einsum('hb,qkb->hqk', table, chooser, precision=HIGHEST, preferred_el...]
    pallas_call x1 -> x4, Pallas kernels: 138 us -> 262 us  [the longest x1 138 us: middle(): pl.pallas_call(middle_kernel, out_shape=shapes, in_specs=[vm] * 14, out_s...]
    psum x2 -> x0, waiting for transfers between devices: 116 us -> none  [the longest x1 115 us: local(): lax.psum((grad_w_query, grad_b_query, grad_w_key, grad_w_value, grad_b_va...]
    psum x1 -> x0, blocking collectives: 24.9 us -> none  [local(): lax.psum((grad_w_query, grad_b_query, grad_w_key, grad_w_value, grad_b_va...]
    add x5 -> x0, other arithmetic: 15.4 us -> none  [the longest x2 12 us: bucket_of(): result = result + (magnitude >= level_start).astype(jnp.int32)]
    reduce_sum x2 -> x0, other arithmetic: 14.1 us -> none  [the longest x1 13.4 us: reading_place(): return (jnp.sum(earlier, axis=2) + order_rank).astype(jnp.int32)]
    unnamed x108 -> x0, local copies, waits for them, and re-layouts: 13.1 us -> none
  transfers between devices with their start and end apart: 2 -> 0, of which waited for: 2 -> 0; matrix products, arithmetic and copies ran while one was open for 10% -> 0% of each run, Pallas kernels for 0% -> 0%
where the time goes in v3:
time: 265 us; the launch traced here: 263 us
  Pallas kernels  262 us (99%)
    pallas_call x1, Pallas kernels, middle(): pl.pallas_call(middle_kernel, out_shape=shapes, in_specs=[vm] * 14, out_s...  138 us
    pallas_call x1, Pallas kernels, tail(): pl.pallas_call(functools.partial(tail_kernel, bits), out_shape=shapes, in...  90.1 us
    pallas_call x1, Pallas kernels, head(): pl.pallas_call(head_kernel, out_shape=shapes, in_specs=[vm] * 15, out_spe...  24.4 us
    pallas_call x1, Pallas kernels, finish(): pl.pallas_call(finish_kernel, out_shape=shapes, in_specs=[hbm] * 5 + [vm]...  9.25 us

profile of v3, /device:TPU:0, one launch (start us, length us, event | category | flops | bytes accessed | tf_op | source)
XLA Modules:
  0.0 262.8 jit_solution(17917923300120501732)
XLA Ops:
  0.7 24.4 %shard_map.410 = (f32[576,768]{1,0:T(8,128)}, f32[576,768]{1,0:T(8,128)}, bf16[640,768]{1,0:T(8,128)(2,1)}, bf16[640,640]{1,0:T(8,128)(2,1)}, bf16[640,256]{1,0:...) custom-call(f32[561,768]{1,0:T(8,128)} %tok.1, ...), custom_call_target="tpu_custom_call" | custom-call | flops 10000000000 | bytes 20971520 | tf_op jit(solution)/shard_map/pallas_call | solution.py:472
  25.1 138.1 %shard_map.411 = (f32[561,768]{1,0:T(8,128)}, f32[576,768]{1,0:T(8,128)}, f32[768,768]{1,0:T(8,128)}, f32[768,768]{1,0:T(8,128)}, f32[8,768]{1,0:T(8,128)}) custom-call(f32[576,768]{1,0:T(8,128)} %get-tuple-element.62.tok_ref, f32[576,768]{1,0:T(8,128)} %get-tuple-element.63.cot_ref, bf16[640,256]{1,0:T(8,128)(2,1)} %get-tuple-element.64.att_ref.att, ...), custom_call_target="tpu_custom_call" | custom-call | flops 4076863488 | bytes 20971520 | tf_op jit(solution)/shard_map/pallas_call | solution.py:320
  163.2 90.1 %shard_map.412 = (f32[561,768]{1,0:T(8,128)}, f32[768,768]{1,0:T(8,128)}, f32[768,768]{1,0:T(8,128)}, f32[768,768]{1,0:T(8,128)}, f32[24,768]{1,0:T(8,128)}) custom-call(f32[576,768]{1,0:T(8,128)} %get-tuple-element.67.gres, f32[8,768]{1,0:T(8,128)} %get-tuple-element.68.small_in, f32[768,768]{1,0:T(8,128)} %get-tuple-element.69.dwi_in, ...), custom_call_target="tpu_custom_call" | custom-call | flops 10000000000 | bytes 20971520 | tf_op jit(solution)/shard_map/pallas_call | solution.py:733
  253.3 9.3 %shard_map.413 = (f32[561,768]{1,0:T(8,128)}, f32[561,768]{1,0:T(8,128)}, f32[192,768]{1,0:T(8,128)}, f32[192,768]{1,0:T(8,128)}, f32[192,768]{1,0:T(8,128)}, /*...) custom-call(f32[561,768]{1,0:T(8,128)} %get-tuple-element.66.out_in,, ...), custom_call_target="tpu_custom_call" | custom-call | tf_op jit(solution)/shard_map/pallas_call | solution.py:781

commit v4 on v3

v4 whole, which is shorter than its diff:
```python
import functools
import math

import jax
import jax.numpy as jnp
import numpy as np
from jax import lax
from jax.experimental import pallas as pl
from jax.experimental.pallas import tpu as pltpu
from jax.sharding import PartitionSpec as P

HEAD_DIM = 64
BINS1 = 32
BINS2 = 64
MAX_ORDER = 128
MAX_LAYOUT = 256
PAGE = 561


HIGHEST = lax.Precision.HIGHEST
EPSILON = 1e-05
SCORE_SCALE = 0.125

def bucket_steps(bins, reach):
    halfway = bins // 2
    exact = halfway // 2
    steps = []
    for level in range(1, halfway):
        if level < exact:
            steps.append(level)
        else:
            found = reach + 1
            for count in range(exact, reach + 2):
                value = exact + int(
                    math.log(count / exact) / math.log(reach / exact) * (halfway - exact)
                )
                if min(value, halfway - 1) >= level:
                    found = count
                    break
            steps.append(found)
    return steps


MESH = pl.DeviceIdType.MESH
BLOCK = 128
PC = 32
LAG = 4


def erf_of(x):
    x = jnp.clip(x, -3.832506856900711, 3.832506856900711)
    s = x * x
    top = -2.72614225801306e-10
    for term in (2.77068142495902e-08, -2.10102402082508e-06, -5.69250639462346e-05,
                 -7.34990630326855e-04, -2.95459980854025e-03, -1.60960333262415e-02):
        top = top * s + term
    low = -1.45660718464996e-05
    for term in (-2.13374055278905e-04, -1.68282697438203e-03, -7.37332916720468e-03,
                 -1.42647390514189e-02):
        low = low * s + term
    return x * top / low


def normal_cdf(x):
    return 0.5 + 0.5 * erf_of(x * math.sqrt(0.5))


def centre(values):
    c = values - jnp.mean(values, axis=-1, keepdims=True)
    r = lax.rsqrt(jnp.mean(c * c, axis=-1, keepdims=True) + EPSILON)
    return c * r, r


def norm_back(g, n, r, gain):
    m = g * gain
    return r * (m - jnp.mean(m, axis=-1, keepdims=True) - n * jnp.mean(m * n, axis=-1, keepdims=True))


def dot_nn(a, b):
    return lax.dot_general(a, b, (((1,), (0,)), ((), ())), preferred_element_type=jnp.float32)


def dot_nt(a, b):
    return lax.dot_general(a, b, (((1,), (1,)), ((), ())), preferred_element_type=jnp.float32)


def dot_tn(a, b):
    return lax.dot_general(a, b, (((0,), (0,)), ((), ())), preferred_element_type=jnp.float32)


class LineSum:
    def __init__(self, part, rx_in, rx_mid, tot, s_in, s_mid, r_in, r_mid):
        self.part, self.rx_in, self.rx_mid, self.tot = part, rx_in, rx_mid, tot
        self.s_in, self.s_mid, self.r_in, self.r_mid = s_in, s_mid, r_in, r_mid
        w, n = lax.axis_index("wide"), lax.axis_index("narrow")
        self.end = (n == 0) | (n == 3)
        self.mid = jnp.logical_not(self.end)
        self.side = (w, n + 1 - 2 * lax.rem(n, 2))
        self.across = (w, 3 - n)
        self.pieces = part.shape[0] // PC

    def rows(self, p):
        return pl.ds(p * PC, PC) if isinstance(p, int) else pl.ds(pl.multiple_of(p * PC, PC), PC)

    def copy_a(self, p):
        return pltpu.make_async_remote_copy(self.part.at[self.rows(p)], self.rx_in.at[self.rows(p)],
            self.s_in.at[p], self.r_in.at[p], device_id=self.side, device_id_type=MESH)

    def copy_b(self, p):
        return pltpu.make_async_remote_copy(self.part.at[self.rows(p)], self.rx_mid.at[self.rows(p)],
            self.s_mid.at[p], self.r_mid.at[p], device_id=self.across, device_id_type=MESH)

    def copy_t(self, p):
        return pltpu.make_async_remote_copy(self.tot.at[self.rows(p)], self.tot.at[self.rows(p)],
            self.s_in.at[p], self.r_in.at[p], device_id=self.side, device_id_type=MESH)

    def signal(self):
        bar = pltpu.get_barrier_semaphore()
        pl.semaphore_signal(bar, inc=1, device_id=self.side, device_id_type=MESH)

        @pl.when(self.mid)
        def _():
            pl.semaphore_signal(bar, inc=1, device_id=self.across, device_id_type=MESH)

    def ready(self, others):
        bar = pltpu.get_barrier_semaphore()

        @pl.when(self.end)
        def _():
            pl.semaphore_wait(bar, 1 + others)

        @pl.when(self.mid)
        def _():
            pl.semaphore_wait(bar, 2 + others)

    def free_part(self, p):
        @pl.when(self.end)
        def _():
            self.copy_a(p).wait_send()

        @pl.when(self.mid)
        def _():
            self.copy_b(p).wait_send()

    def finish(self, p, first):
        self.copy_b(p).wait_recv()
        if not first:
            self.copy_t(p).wait_send()
        self.tot[self.rows(p), :] = self.part[self.rows(p), :] + self.rx_mid[self.rows(p), :]
        self.copy_t(p).start()

    def slot(self, p, order, done=None):
        @pl.when(self.end)
        def _():
            self.copy_a(p).start()

        @pl.when(self.mid)
        def _():
            self.copy_a(p).wait_recv()
            self.part[self.rows(p), :] += self.rx_in[self.rows(p), :]
            self.copy_b(p).start()

            if done is not None:
                for q in done:
                    self.finish(q, order == 0)
                return

            @pl.when(p >= LAG)
            def _():
                self.finish(p - LAG, order == 0)

            if order > 0:
                @pl.when(p < LAG)
                def _():
                    self.finish(p + self.pieces - LAG, order == 1)

    def send_end(self, p):
        @pl.when(self.end)
        def _():
            self.copy_a(p).start()

    def slot_mid(self, p, done):
        @pl.when(self.mid)
        def _():
            self.copy_a(p).wait_recv()
            self.part[self.rows(p), :] += self.rx_in[self.rows(p), :]
            self.copy_b(p).start()
            for q in done:
                self.finish(q, False)

    def last(self, pieces):
        @pl.when(self.mid)
        def _():
            for q in pieces:
                self.finish(q, False)

    def want(self, p):
        @pl.when(self.end)
        def _():
            self.copy_t(p).wait_recv()

    def drain(self):
        def one(p, c):
            self.free_part(p)

            @pl.when(self.mid)
            def _():
                self.copy_t(p).wait_send()
            return c
        lax.fori_loop(0, self.pieces, one, 0)


WIDE_ROWS = 640
ROWS = 576


def bucket_number(offset, bins, reach):
    halfway = bins // 2
    steps = bucket_steps(bins, reach)
    return (halfway if offset > 0 else 0) + sum(1 for s in steps if abs(offset) >= s)


def choose_matrix(offsets, bins, reach):
    out = np.zeros((bins, len(offsets)), np.float32)
    for place, offset in enumerate(offsets):
        out[bucket_number(offset, bins, reach), place] = 1.0
    return out


def split3(x):
    hi = x.astype(jnp.bfloat16)
    rest = x - hi.astype(jnp.float32)
    mid = rest.astype(jnp.bfloat16)
    return hi, mid, (rest - mid.astype(jnp.float32)).astype(jnp.bfloat16)


def split2(x):
    hi = x.astype(jnp.bfloat16)
    return hi, (x - hi.astype(jnp.float32)).astype(jnp.bfloat16)


def exact_dot(a, b, dims):
    return lax.dot_general(a, b, (dims, ((), ())), precision=HIGHEST, preferred_element_type=jnp.float32)


def lanes_of(h, shape):
    lane = lax.broadcasted_iota(jnp.int32, shape, 1)
    return (lane >= h * HEAD_DIM) & (lane < (h + 1) * HEAD_DIM)


def block_rows(m, n):
    return pl.ds(m * BLOCK, n) if isinstance(m, int) else pl.ds(pl.multiple_of(m * BLOCK, BLOCK), n)


def block_window(m):
    start = 512 - m * BLOCK
    return pl.ds(start if isinstance(m, int) else pl.multiple_of(start, 128), WIDE_ROWS)


class CubeSum:
    def __init__(self, ref, rx1, rx2, rx3, rx4, rxb, ssem, rsem, free, bits):
        self.ref, self.rx1, self.rx2, self.rx3, self.rx4, self.rxb = ref, rx1, rx2, rx3, rx4, rxb
        self.ssem, self.rsem, self.free = ssem, rsem, free
        w, n = lax.axis_index("wide"), lax.axis_index("narrow")
        self.bit = [lax.rem(lax.div(w, 2 ** i), 2) for i in range(bits)]
        self.to = [(w + 2 ** i * (1 - 2 * self.bit[i]), n) for i in range(bits)]
        self.rows = ref.shape[0]
        half = self.rows // 2
        self.half, self.stream, self.eighth, self.piece = half, half // 2, half // 4, half // 8
        self.own = self.bit[0] * half
        self.axes = ((1, 2), (2, 1))
        self.extra = range(3, bits)

    def at(self, start, size):
        return pl.ds(pl.multiple_of(start, self.piece), size)

    def base1(self, s, other):
        b = self.bit[self.axes[s][0]]
        b = 1 - b if other else b
        return self.own + s * self.stream + b * self.eighth

    def base2(self, s, other):
        b = self.bit[self.axes[s][1]]
        b = 1 - b if other else b
        return self.base1(s, False) + b * self.piece

    def copy(self, src, dst, i, axis):
        return pltpu.make_async_remote_copy(src, dst, self.ssem.at[i], self.rsem.at[i], device_id=self.to[axis],
                                            device_id_type=MESH)

    def core_out(self):
        return self.copy(self.ref.at[self.at((1 - self.bit[0]) * self.half, self.half)], self.rx1, 0, 0)

    def first(self, s):
        return self.copy(self.ref.at[self.at(self.base1(s, True), self.eighth)], self.rx2[s], 1 + s, self.axes[s][0])

    def second(self, s):
        return self.copy(self.ref.at[self.at(self.base2(s, True), self.piece)], self.rx3[s], 3 + s, self.axes[s][1])

    def back2(self, s):
        r = self.at(self.base2(s, False), self.piece)
        return self.copy(self.ref.at[r], self.rxb[s], 5 + s, self.axes[s][1])

    def back1(self, s):
        r = self.at(self.base1(s, False), self.eighth)
        return self.copy(self.ref.at[r], self.ref.at[r], 7 + s, self.axes[s][0])

    def core_back(self):
        r = self.at(self.own, self.half)
        return self.copy(self.ref.at[r], self.ref.at[r], 9, 0)

    def more(self, e, s):
        i = e - 3
        return self.copy(self.ref.at[self.at(self.base2(s, False), self.piece)], self.rx4.at[i, s], 10 + 2 * i + s, e)

    def release(self, i, axis):
        pl.semaphore_signal(self.free.at[i], inc=1, device_id=self.to[axis], device_id_type=MESH)

    def step(self, i):
        if i == 0:
            self.core_out().start()
        if i == 1:
            self.core_out().wait_recv()
            self.ref[self.at(self.own, self.half), :] += self.rx1[...]
            for s in range(2):
                self.first(s).start()
            self.core_out().wait_send()
            self.release(0, 0)
        if i == 2:
            for s in range(2):
                self.first(s).wait()
                self.release(1 + s, self.axes[s][0])
                self.ref[self.at(self.base1(s, False), self.eighth), :] += self.rx2[s][...]
                self.second(s).start()
        if i == 3:
            for s in range(2):
                self.second(s).wait()
                self.ref[self.at(self.base2(s, False), self.piece), :] += self.rx3[s][...]
            for e in self.extra:
                for s in range(2):
                    self.more(e, s).start()
                for s in range(2):
                    self.more(e, s).wait()
                    self.ref[self.at(self.base2(s, False), self.piece), :] += self.rx4[e - 3, s]
            for s in range(2):
                self.back2(s).start()
        if i == 4:
            for s in range(2):
                self.back2(s).wait_recv()
                self.ref[self.at(self.base2(s, True), self.piece), :] = self.rxb[s][...]
                pl.semaphore_wait(self.free.at[1 + s], 1)
                self.back1(s).start()
        if i == 5:
            for s in range(2):
                self.back1(s).wait_recv()
            pl.semaphore_wait(self.free.at[0], 1)
            self.core_back().start()
        if i == 6:
            self.core_back().wait()
            for s in range(2):
                self.back2(s).wait_send()
                self.back1(s).wait_send()


def layer_kernel(bits, tok_h, cot_h, wq_h, wk_h, wv_h, wo_h, wi_h, wd_h, reg, rank, box, bq, bv, bo_r, g1_r, b1_r, bi_r, bd_r, g2_r, b2_r,
                 to, tx, ty, so, sxy, sgo, sgxy,
                 out_h, gin_h, gat_h, gwi_h, gwd_h, sm,
                 out, gin, gat, gwi, gwd, part, rx_in, rx_mid, tot, res, cotp, hid, pre, act, gff, hlow, gpre, low, perm,
                 q_s, k_s, v_s, prob, att, ob, obf, pairs, ob4, split_s, base, ga, gt, qt, dkt, dvt, dq, dk, dv, gacc,
                 ws, wo, wi, wd, outp, rows_s, vec_s, rx1, rx2, rx3, rx4, rxb, rxs,
                 s_in, s_mid, r_in, r_mid, cs, cr, cf, ss, sr, ls):
    f32, bf = jnp.float32, jnp.bfloat16
    n = PAGE
    width = wo_h.shape[0]
    heads = to.shape[0]
    block_pieces = BLOCK // PC
    line = LineSum(part, rx_in, rx_mid, tot, s_in, s_mid, r_in, r_mid)
    pieces = line.pieces
    closing = {p: [p - LAG] for p in range(LAG, pieces)}
    closing[pieces - 2] = [pieces - 6, pieces - 5]
    closing[pieces - 1] = [pieces - 4, pieces - 3]
    rest1, rest2, rest3, restb = pre.at[pl.ds(0, 384)], pre.at[pl.ds(384, 192)], cotp.at[pl.ds(0, 96)], cotp.at[pl.ds(96, 96)]
    cube = [CubeSum(gwi, rx1.at[0], [rx2.at[0, s] for s in range(2)], [rx3.at[0, s] for s in range(2)], rx4.at[0],
                    [rxb.at[0, s] for s in range(2)], cs.at[0], cr.at[0], cf.at[0], bits),
            CubeSum(gwd, rx1.at[1], [rx2.at[1, s] for s in range(2)], [rx3.at[1, s] for s in range(2)], rx4.at[1],
                    [rxb.at[1, s] for s in range(2)], cs.at[1], cr.at[1], cf.at[1], bits),
            CubeSum(gat, rest1, [pre.at[pl.ds(384 + 96 * s, 96)] for s in range(2)],
                    [cotp.at[pl.ds(48 * s, 48)] for s in range(2)], rx4.at[2],
                    [cotp.at[pl.ds(96 + 48 * s, 48)] for s in range(2)], cs.at[2], cr.at[2], cf.at[2], bits)]

    def load(i, src, dst):
        return pltpu.make_async_copy(src, dst, ls.at[i])
    loads = [load(0, tok_h, out)]
    loads += [load(1 + i, src, gat.at[pl.ds(i * width, width)]) for i, src in enumerate((wq_h, wk_h, wv_h, wo_h))]
    loads += [load(5, wi_h, gwi), load(6, wd_h, gwd), load(7, cot_h, gin)]
    for c in loads:
        c.start()
    bar = pltpu.get_barrier_semaphore()
    for peer in cube[0].to:
        pl.semaphore_signal(bar, inc=1, device_id=peer, device_id_type=MESH)
    line.signal()

    rows_s[...] = jnp.full(rows_s.shape, 1e4, f32)
    rows_s[0, 0:n] = reg[...].astype(f32)
    rows_s[1, 0:n] = rank[...].astype(f32)
    rows_s[2:4, 0:n] = box[...].astype(f32)
    region_row, rank_row = rows_s[0:1, :], rows_s[1:2, :]
    i0 = lax.broadcasted_iota(jnp.int32, (WIDE_ROWS, WIDE_ROWS), 0)
    i1 = lax.broadcasted_iota(jnp.int32, (WIDE_ROWS, WIDE_ROWS), 1)
    region_col = jnp.sum(jnp.where(i0 == i1, region_row, 0.0), axis=1, keepdims=True)
    place = jnp.sum(jnp.where(region_col < region_row, 1.0, 0.0), axis=0, keepdims=True) + rank_row
    perm[...] = jnp.where(i0.astype(f32) == place, 1.0, 0.0).astype(bf)
    split_s[...] = jnp.zeros_like(split_s)
    for i, vector in enumerate((bo_r, g1_r, b1_r, bi_r, bd_r, g2_r, b2_r)):
        vec_s[i, :] = vector[...]
    vec_s[7:9, :] = jnp.zeros((2, vec_s.shape[1]), f32)
    vec_s[7, 0:width] = bq[...]
    vec_s[8, 0:width] = bv[...]
    b_out, g1, b1, b_in, b_down, g2, b2 = (vec_s[i:i + 1, :] for i in range(7))

    def sort_first(source, target, first):
        split_s[0:n, :] = source[...].astype(bf)
        y = dot_nn(perm[...], split_s[...])
        if first is not None:
            first[...] = y.astype(bf)
        target[...] = y[0:ROWS, :]

    def sort_rest(source, target):
        for i in range(1, 3):
            split_s[0:n, :] = split3(source[...])[i]
            target[...] += dot_nn(perm[0:ROWS, :], split_s[...])

    loads[0].wait()
    sort_first(out, res, low)
    code = lax.broadcasted_iota(jnp.int32, (128, WIDE_ROWS), 0).astype(f32)
    for i in range(2):
        row = rows_s[2 + i:3 + i, :]
        one = dot_nt(perm[...], jnp.where(code == row, 1.0, 0.0).astype(bf)).astype(bf)
        ob[:, 128 * i:128 * (i + 1)] = one
        ob4[:, 256 * i:256 * i + 128] = one
        ob4[:, 256 * i + 128:256 * i + 256] = one
        obf[:, 128 * i:128 * (i + 1)] = dot_nt(perm[...], jnp.where(127.0 - code == row, 1.0, 0.0).astype(bf)).astype(bf)
    ws[...] = jnp.zeros_like(ws)
    for i in range(3):
        loads[1 + i].wait()
        ws[i, 0:width, :] = gat[i * width:(i + 1) * width, :].astype(bf)
    q_s[...] = ((dot_nt(low[...], ws[0]) + vec_s[7:8, 0:256]).astype(bf) * SCORE_SCALE).astype(bf)
    k_s[...] = dot_nt(low[...], ws[1]).astype(bf)
    v_s[...] = (dot_nt(low[...], ws[2]) + vec_s[8:9, 0:256]).astype(bf)
    wo[...] = jnp.zeros_like(wo)
    loads[4].wait()
    wo[0:width, :] = gat[3 * width:4 * width, :].astype(bf)
    row_o = exact_dot(to[...], so[...], ((1,), (0,)))
    row_xy = (exact_dot(tx[...], sxy[...], ((1,), (0,))), exact_dot(ty[...], sxy[...], ((1,), (0,))))
    for h in range(heads):
        base[h] = pltpu.roll(jnp.broadcast_to(row_o[h:h + 1, :], (128, 1280)), 0, 1, stride=1, stride_axis=0)
        for i in range(2):
            table = pltpu.roll(jnp.broadcast_to(row_xy[i][h:h + 1, :], (128, 256)), 0, 1, stride=1, stride_axis=0)
            pairs[h, i] = jnp.concatenate(split2(table[:, 0:128]), axis=1)
    line.ready(bits)

    def blocks(body, start=0):
        full = ROWS // BLOCK

        def step(m, carry):
            body(m, BLOCK)
            return carry
        lax.fori_loop(start, full, step, 0)
        if ROWS % BLOCK:
            body(full, ROWS % BLOCK)

    def sends(m, rows, order):
        for j in range(rows // PC):
            p = m * block_pieces + j
            line.slot(p, order, closing[p] if order == 2 and isinstance(p, int) else None)

    def attend(m, rows):
        r = block_rows(m, rows)
        mixed = None
        for h in range(heads):
            qh = jnp.where(lanes_of(h, (rows, 256)), q_s[r, :], jnp.zeros((), bf))
            bias = jnp.concatenate([dot_nn(ob[r, 128 * i:128 * (i + 1)], pairs[h, i]).astype(bf) for i in range(2)], axis=1)
            s = dot_nt(qh, k_s[...]) + dot_nt(bias, ob4[...]) + base[h, 0:rows, block_window(m)]
            s = jnp.where(lax.broadcasted_iota(jnp.int32, s.shape, 1) < n, s, -1e30)
            e = jnp.exp(s - jnp.max(s, axis=1, keepdims=True))
            p = e / jnp.sum(e, axis=1, keepdims=True)
            prob[h, r, :] = p
            pv = dot_nn(p.astype(bf), v_s[...])
            mixed = pv if h == 0 else jnp.where(lanes_of(h, (rows, 256)), pv, mixed)
        mixed = mixed.astype(bf)
        att[r, :] = mixed
        part[r, :] = dot_nn(mixed, wo[...])
        sends(m, rows, 0)
    blocks(attend)

    sort_rest(out, res)
    loads[5].wait()
    wi[...] = gwi[...].astype(bf)
    loads[6].wait()
    wd[...] = gwd[...].astype(bf)
    sm[...] = jnp.zeros_like(sm)

    def open_block(m, rows):
        for j in range(rows // PC):
            line.want(m * block_pieces + j)
        for j in range(rows // PC):
            line.free_part(m * block_pieces + j)

    def forward(m, rows):
        r = block_rows(m, rows)
        open_block(m, rows)
        one = res[r, :] + (tot[r, :] + b_out)
        res[r, :] = one
        c, _ = centre(one)
        hidden = c * g1 + b1
        hid[r, :] = hidden
        hl = hidden.astype(bf)
        hlow[r, :] = hl
        u = dot_nn(hl, wi[...]) + b_in
        pre[r, :] = u
        a = (u * normal_cdf(u)).astype(bf)
        act[r, :] = a
        part[r, :] = dot_nn(a, wd[...])
        sends(m, rows, 1)
    blocks(forward)

    loads[7].wait()
    sort_first(gin, cotp, None)
    sort_rest(gin, cotp)
    outp[...] = jnp.zeros_like(outp)
    qt[...] = jnp.transpose(q_s[...])
    dkt[...] = jnp.zeros_like(dkt)
    dvt[...] = jnp.zeros_like(dvt)
    base[...] = jnp.zeros_like(base)
    gacc[...] = jnp.zeros_like(gacc)
    ga[...] = jnp.zeros_like(ga)
    dq[...] = jnp.zeros_like(dq)
    gat[3 * width:4 * width, :] = jnp.zeros((width, gat.shape[1]), f32)

    def add_row(i, value):
        sm[i:i + 1, :] += jnp.sum(value, axis=0, keepdims=True)

    def put_back(r, y):
        total = outp[...]
        for piece in split3(y):
            total = total + dot_tn(perm[r, :], piece)
        outp[...] = total

    def back(m, rows):
        r = block_rows(m, rows)
        open_block(m, rows)
        two = hid[r, :] + (tot[r, :] + b_down)
        c, rs = centre(two)
        g = cotp[r, :]
        add_row(0, g * c)
        add_row(1, g)
        gradient = norm_back(g, c, rs, g2)
        hid[r, :] = gradient
        gl = gradient.astype(bf)
        gff[r, :] = gl
        add_row(2, gl.astype(f32))
        slope_in = dot_nt(gl, wd[...])
        u = pre[r, :]
        slope = normal_cdf(u) + u * (jnp.exp(-0.5 * u * u) * (1.0 / math.sqrt(2.0 * math.pi)))
        gp = (slope_in * slope).astype(bf)
        gpre[r, :] = gp
        add_row(3, gp.astype(f32))
        part[r, :] = dot_nt(gp, wi[...])
        sends(m, rows, 2)
        put_back(r, c * g2 + b2)

    def attend_back(m, rows):
        r = block_rows(m, rows)
        for j in range(rows // PC):
            line.want(m * block_pieces + j)
        g = hid[r, :] + tot[r, :]
        c, rs = centre(res[r, :])
        add_row(4, g * c)
        add_row(5, g)
        gradient = norm_back(g, c, rs, g1)
        hid[r, :] = gradient
        gb = gradient.astype(bf)
        add_row(6, gb.astype(f32))
        gat[3 * width:4 * width, :] += dot_tn(att[r, :], gb)[0:width, :]
        gab = dot_nt(gb, wo[...]).astype(bf)
        ga[0:rows, :] = gab
        gt[...] = jnp.transpose(ga[...])
        cols = pl.ds(pl.multiple_of(m * BLOCK, BLOCK), rows)
        query_grad = None
        for h in range(heads):
            gh = jnp.where(lanes_of(h, (rows, 256)), gab, jnp.zeros((), bf))
            dp = dot_nt(gh, v_s[...])
            p = prob[h, r, :]
            inner = jnp.sum(p * dp, axis=1, keepdims=True)
            ds = (p * (dp - inner)).astype(bf)
            dqh = dot_nn(ds, k_s[...])
            query_grad = dqh if h == 0 else jnp.where(lanes_of(h, (rows, 256)), dqh, query_grad)
            base[h, 0:rows, block_window(m)] += ds.astype(f32)
            hr = pl.ds(h * HEAD_DIM, HEAD_DIM)
            dkt[hr, :] += dot_nn(qt[hr, cols], ds)
            dvt[hr, :] += dot_nn(gt[hr, 0:rows], p.astype(bf))
            u = jnp.concatenate(split2(dot_nn(ds, ob[...])), axis=1)
            gg = dot_tn(obf[r, :], u)
            for i in range(2):
                b = 128 * i
                gacc[h, i] += gg[b:b + 128, b:b + 128] + gg[b:b + 128, 256 + b:384 + b]
        dq[r, :] = jnp.where(lax.broadcasted_iota(jnp.int32, (rows, 256), 1) < width, query_grad * SCORE_SCALE, 0.0).astype(bf)

    def back_step(m, carry):
        back(m, BLOCK)

        @pl.when(m == ROWS // BLOCK - 1)
        def _():
            attend_back(0, BLOCK)
        return carry
    lax.fori_loop(0, ROWS // BLOCK, back_step, 0)
    back(ROWS // BLOCK, ROWS % BLOCK)

    def late_step(m, carry):
        @pl.when(m == 2)
        def _():
            line.last([pieces - 2, pieces - 1])
            gwd[...] = dot_tn(act[...], gff[...])
            cube[1].step(0)
            gwi[...] = dot_tn(hlow[...], gpre[...])
            cube[0].step(0)
        attend_back(m, BLOCK)
        return carry
    lax.fori_loop(1, ROWS // BLOCK, late_step, 0)
    out[...] = outp[0:n, :]
    store_out = [pltpu.make_async_copy(a, b, ls.at[i]) for i, (a, b) in enumerate(((out, out_h), (gwd, gwd_h), (gwi, gwi_h), (gat, gat_h), (gin, gin_h)))]
    store_out[0].start()
    outp[...] = jnp.zeros_like(outp)
    attend_back(ROWS // BLOCK, ROWS % BLOCK)
    dk[...] = jnp.transpose(dkt[...]).astype(bf)
    dv[...] = jnp.transpose(dvt[...]).astype(bf)
    cube[1].step(1)
    cube[0].step(1)

    def produce(m, rows):
        r = block_rows(m, rows)
        for j in range(rows // PC):
            line.free_part(m * block_pieces + j)
        part[r, :] = dot_nn(dq[r, :], ws[0]) + dot_nn(dk[r, :], ws[1]) + dot_nn(dv[r, :], ws[2])
        for j in range(rows // PC):
            line.send_end(m * block_pieces + j)
    blocks(produce)

    def table_sums(h):
        for i in range(2):
            both = jnp.concatenate([gacc[h, i], jnp.zeros((128, 128), f32)], axis=1)
            line_sum = jnp.sum(pltpu.roll(both, 0, 1, stride=1, stride_axis=0), axis=0, keepdims=True)
            sm[10 + heads * (i + 1) + h:11 + heads * (i + 1) + h, 0:BINS2] = exact_dot(line_sum, sgxy[...], ((1,), (1,)))
        flip = (lax.broadcasted_iota(jnp.int32, (128, 128), 0) + lax.broadcasted_iota(jnp.int32, (128, 128), 1)) == 127
        flip = jnp.where(flip, 1.0, 0.0).astype(bf)
        hi, lo = split2(base[h])
        turned = dot_nn(flip, hi) + dot_nn(flip, lo)
        line_sum = jnp.sum(pltpu.roll(turned, 0, 1, stride=1, stride_axis=0), axis=0, keepdims=True)
        sm[10 + h:11 + h, 0:BINS1] = exact_dot(line_sum, sgo[...], ((1,), (1,)))

    def bias_sums(_):
        sm[8:9, 0:256] = jnp.sum(dq[...].astype(f32), axis=0, keepdims=True)
        sm[9:10, 0:256] = jnp.sum(dv[...].astype(f32), axis=0, keepdims=True)

    bit_to = cube[0].to

    def small_copy(i):
        return pltpu.make_async_remote_copy(sm, rxs.at[i], ss.at[i], sr.at[i], device_id=bit_to[i], device_id_type=MESH)

    def small_step(i):
        if i > 0:
            small_copy(i - 1).wait()
            sm[...] += rxs[i - 1]
        if i < bits:
            small_copy(i).start()

    def weight_grad(i):
        gat[i * width:(i + 1) * width, :] = dot_tn((dq, dk, dv)[i][...], low[...])[0:width, :]

    def consume(m):
        rows = min(BLOCK, ROWS - m * BLOCK)
        for j in range(rows // PC):
            line.want(m * block_pieces + j)
        r = slice(m * BLOCK, m * BLOCK + rows)
        put_back(r, hid[r, :] + tot[r, :])

    def both_step(i):
        cube[1].step(i)
        cube[0].step(i)
    jobs = {0: [(weight_grad, 0)], 1: [(weight_grad, 1)], 2: [(weight_grad, 2)], 3: [(cube[2].step, 0)], 4: [(both_step, 2), (bias_sums, 0)],
            5: [(cube[2].step, 1), (table_sums, 0)], 6: [(table_sums, 1)], 7: [(table_sums, 2), (small_step, 0)],
            8: [(both_step, 3)], 9: [(cube[2].step, 2), (small_step, 1)], 10: [(consume, 0)], 11: [(both_step, 4), (small_step, 2)],
            12: [(cube[2].step, 3)], 13: [(small_step, 3)], 14: [(consume, 1), (cube[2].step, 4)], 17: [(both_step, 5)]}
    ending = {p: [p - LAG] for p in range(LAG, pieces - 4)}
    ending.update({pieces - 4: [pieces - 8, pieces - 7], pieces - 3: [pieces - 6], pieces - 2: [pieces - 5, pieces - 4],
                   pieces - 1: [pieces - 3, pieces - 2]})
    for p in range(pieces):
        line.slot_mid(p, ending.get(p, ()))
        for job, arg in jobs.get(p, ()):
            job(arg)
    line.last([pieces - 1])
    for i in range(4, bits + 1):
        small_step(i)
    consume(2)
    cube[2].step(5)
    consume(3)
    both_step(6)
    store_out[1].start()
    store_out[2].start()
    cube[2].step(6)
    store_out[3].start()
    consume(4)
    gin[...] = outp[0:n, :]
    store_out[4].start()
    line.drain()
    for c in store_out:
        c.wait()


def layer(bits, tok, cot, wq, wk, wv, wo, wi, wd, *small_args):
    f32, bf = jnp.float32, jnp.bfloat16
    d = tok.shape[1]
    f = wi.shape[1]
    width = wo.shape[0]
    heads = small_args[12].shape[0]
    sd = jax.ShapeDtypeStruct
    W, R = WIDE_ROWS, ROWS
    pieces = R // PC
    more = max(bits - 3, 1)
    vm, hbm = pl.BlockSpec(memory_space=pltpu.VMEM), pl.BlockSpec(memory_space=pl.ANY)
    v_ = pltpu.VMEM
    shapes = (sd((PAGE, d), f32), sd((PAGE, d), f32), sd((4 * width, d), f32), sd((d, f), f32), sd((f, d), f32), sd((24, d), f32))
    scratch = [v_(s.shape, f32) for s in shapes[:5]]
    scratch += [v_((R, d), f32)] * 7 + [v_((R, f), f32), v_((R, f), bf), v_((R, d), bf), v_((R, d), bf), v_((R, f), bf)]
    scratch += [v_((W, d), bf), v_((W, W), bf)] + [v_((W, 256), bf)] * 3 + [v_((heads, R, W), f32)] + [v_((W, 256), bf)] * 3
    scratch += [v_((heads, 2, 128, 256), bf), v_((W, 512), bf), v_((W, d), bf), v_((heads, 128, 1280), f32)]
    scratch += [v_((BLOCK, 256), bf), v_((256, BLOCK), bf), v_((256, W), bf), v_((256, W), f32), v_((256, W), f32)]
    scratch += [v_((W, 256), bf)] * 3 + [v_((heads, 2, 128, 128), f32)]
    scratch += [v_((3, 256, d), bf), v_((256, d), bf), v_((d, f), bf), v_((f, d), bf), v_((W, d), f32), v_((8, W), f32), v_((16, d), f32)]
    scratch += [v_((2, d // 2, d), f32), v_((2, 2, d // 8, d), f32), v_((2, 2, d // 16, d), f32), v_((3, more, 2, d // 16, d), f32),
                v_((2, 2, d // 16, d), f32), v_((bits, 24, d), f32)]
    scratch += [pltpu.SemaphoreType.DMA((pieces,))] * 4 + [pltpu.SemaphoreType.DMA((3, 10 + 2 * more))] * 2
    scratch += [pltpu.SemaphoreType.REGULAR((3, 3))] + [pltpu.SemaphoreType.DMA((bits,))] * 2 + [pltpu.SemaphoreType.DMA((8,))]
    return pl.pallas_call(
        functools.partial(layer_kernel, bits), out_shape=shapes, in_specs=[hbm] * 8 + [vm] * 19, out_specs=[hbm] * 5 + [vm],
        scratch_shapes=scratch,
        compiler_params=pltpu.CompilerParams(collective_id=0, has_side_effects=True, vmem_limit_bytes=62 << 20),
        cost_estimate=pl.CostEstimate(flops=3 * 10 ** 10, bytes_accessed=20 << 20, transcendentals=heads * R * W),
    )(tok, cot, wq, wk, wv, wo, wi, wd, *small_args)


def finish_kernel(out_in, gin_in, gat_in, gwi_in, gwd_in, sm, out, gin, gwq, gwk, gwv, gwo, gwi, gwd, *rest):
    vectors, (b_out, b_gin, b_gat, b_gwi, b_gwd, sem_in, sem_out) = rest[:12], rest[12:]
    width = gwo.shape[0]
    heads = vectors[9].shape[0]
    whole = [(out_in, b_out, out), (gin_in, b_gin, gin), (gwi_in, b_gwi, gwi), (gwd_in, b_gwd, gwd)]
    for i, g in enumerate((gwq, gwk, gwv, gwo)):
        r = pl.ds(i * width, width)
        whole.append((gat_in.at[r], b_gat.at[r], g))
    inward = [pltpu.make_async_copy(a, b, sem_in.at[i]) for i, (a, b, _) in enumerate(whole)]
    outward = [pltpu.make_async_copy(b, c, sem_out.at[i]) for i, (_, b, c) in enumerate(whole)]
    for c in inward:
        c.start()
    for i in range(7):
        vectors[i][...] = sm[i, :]
    vectors[7][...] = sm[8, 0:width]
    vectors[8][...] = sm[9, 0:width]
    vectors[9][...] = sm[10:10 + heads, 0:BINS1]
    vectors[10][...] = sm[10 + heads:10 + 2 * heads, 0:BINS2]
    vectors[11][...] = sm[10 + 2 * heads:10 + 3 * heads, 0:BINS2]
    for c, o in zip(inward, outward):
        c.wait()
        o.start()
    for o in outward:
        o.wait()


def finish(heads, width, out, gin, gat, gwi, gwd, sm):
    f32 = jnp.float32
    sd = jax.ShapeDtypeStruct
    d = gat.shape[1]
    like = lambda x: sd(x.shape, f32)
    shapes = (like(out), like(gin)) + (sd((width, d), f32),) * 4 + (like(gwi), like(gwd)) + (sd((d,), f32),) * 7 \
        + (sd((width,), f32),) * 2 + (sd((heads, BINS1), f32), sd((heads, BINS2), f32), sd((heads, BINS2), f32))
    vm, hbm = pl.BlockSpec(memory_space=pltpu.VMEM), pl.BlockSpec(memory_space=pl.ANY)
    return pl.pallas_call(
        finish_kernel, out_shape=shapes, in_specs=[hbm] * 5 + [vm], out_specs=[hbm] * 8 + [vm] * 12,
        scratch_shapes=[pltpu.VMEM(x.shape, f32) for x in (out, gin, gat, gwi, gwd)] + [pltpu.SemaphoreType.DMA((8,))] * 2,
        compiler_params=pltpu.CompilerParams(vmem_limit_bytes=56 << 20),
    )(out, gin, gat, gwi, gwd, sm)


def local(
    bits,
    tokens,
    region,
    order_rank,
    box_coords,
    w_query,
    b_query,
    w_key,
    w_value,
    b_value,
    w_out,
    b_out,
    ln1_gain,
    ln1_bias,
    w_in,
    b_in,
    w_down,
    b_down,
    ln2_gain,
    ln2_bias,
    rel_order,
    rel_x,
    rel_y,
    cotangent,
):
    so = choose_matrix([i - 512 if i < 1152 else i - 1792 for i in range(1280)], BINS1, MAX_ORDER)
    sxy = choose_matrix([i if i < 128 else i - 256 for i in range(256)], BINS2, MAX_LAYOUT)
    sgo = choose_matrix([i - 639 for i in range(1280)], BINS1, MAX_ORDER)
    sgxy = choose_matrix([i - 127 for i in range(256)], BINS2, MAX_LAYOUT)
    width = w_out.shape[0]
    heads = rel_order.shape[0]
    output, gin, gat, gwi, gwd, sm = layer(
        bits, tokens, cotangent, w_query.T, w_key.T, w_value.T, w_out, w_in, w_down, region, order_rank, box_coords, b_query, b_value,
        b_out, ln1_gain, ln1_bias, b_in, b_down, ln2_gain, ln2_bias, rel_order, rel_x, rel_y, so, sxy, sgo, sgxy)
    (output, gin, gwq, gwk, gwv, gwo, gwi, gwd, l2g, l2b, bd, bi, l1g, l1b, bo, gbq, gbv, ro, rx, ry) = finish(
        heads, width, output, gin, gat, gwi, gwd, sm)
    return (output, gin, gwq.T, gbq, gwk.T, gwv.T, gbv, gwo, bo, l1g, l1b, gwi, bi,
            gwd, bd, l2g, l2b, ro, rx, ry)


def solution(mesh):
    in_specs = (
        P("wide", None),
        P("wide"),
        P("wide"),
        P(None, "wide"),
        P(None, "narrow"),
        P("narrow"),
        P(None, "narrow"),
        P(None, "narrow"),
        P("narrow"),
        P("narrow", None),
        P(),
        P(),
        P(),
        P(None, "narrow"),
        P("narrow"),
        P("narrow", None),
        P(),
        P(),
        P(),
        P("narrow", None),
        P("narrow", None),
        P("narrow", None),
        P("wide", None),
    )
    out_specs = (
        P("wide", None),
        P("wide", None),
        P(None, "narrow"),
        P("narrow"),
        P(None, "narrow"),
        P(None, "narrow"),
        P("narrow"),
        P("narrow", None),
        P(),
        P(),
        P(),
        P(None, "narrow"),
        P("narrow"),
        P("narrow", None),
        P(),
        P(),
        P(),
        P("narrow", None),
        P("narrow", None),
        P("narrow", None),
    )
    bits = mesh.shape["wide"].bit_length() - 1
    return jax.shard_map(functools.partial(local, bits), mesh=mesh, in_specs=in_specs, out_specs=out_specs, check_vma=False)
```

time: 265 us -> 227 us (0.86)
  Pallas kernels: 262 us -> 226 us
    pallas_call x3 -> x1, Pallas kernels: 253 us -> 217 us  [layer(): pl.pallas_call(functools.partial(layer_kernel, bits), out_shape=shapes, i...]
where the time goes in v4:
time: 227 us
  Pallas kernels  226 us (100%)
    pallas_call x1, Pallas kernels, layer(): pl.pallas_call(functools.partial(layer_kernel, bits), out_shape=shapes, i...  217 us
    pallas_call x1, Pallas kernels, finish(): pl.pallas_call(finish_kernel, out_shape=shapes, in_specs=[hbm] * 5 + [vm]...  9.25 us

profile of v4, /device:TPU:0, one launch (start us, length us, event | category | flops | bytes accessed | tf_op | source)
XLA Modules:
  0.0 227.1 jit_solution(11464119110992284367)
XLA Ops:
  0.7 217.0 %shard_map.410 = (f32[561,768]{1,0:T(8,128)}, f32[561,768]{1,0:T(8,128)}, f32[768,768]{1,0:T(8,128)}, f32[768,768]{1,0:T(8,128)}, f32[768,768]{1,0:T(8,128)}, /*index=5*/f32[24,768]{1,0:T(8,128)}) custom-call(f32[561,768]{1,0:T(8,128)} %tok_h.1, f32[561,768]{1,0:T(8,128)} %cot_h.1, f32[192,768]{1,0:T(8,128)} %bitcast.6, f32[192,768]{1,0:T(8,128)} %bitcast.7, ...), custom_call_target="tpu_custom_call" | custom-call | flops 30000001024 | bytes 20971520 | tf_op jit(solution)/shard_map/pallas_call | solution.py:744
  217.6 9.3 %shard_map.411 = (f32[561,768]{1,0:T(8,128)}, f32[561,768]{1,0:T(8,128)}, f32[192,768]{1,0:T(8,128)}, f32[192,768]{1,0:T(8,128)}, f32[192,768]{1,0:T(8,128)}, /*...) custom-call(f32[561,768]{1,0:T(8,128)} %get-tuple-element.46.out_in,, ...), custom_call_target="tpu_custom_call" | custom-call | tf_op jit(solution)/shard_map/pallas_call | solution.py:786

commit v5 on v4

--- a/solution.py
+++ b/solution.py
@@ -364,8 +364,8 @@
 
 def layer_kernel(bits, tok_h, cot_h, wq_h, wk_h, wv_h, wo_h, wi_h, wd_h, reg, rank, box, bq, bv, bo_r, g1_r, b1_r, bi_r, bd_r, g2_r, b2_r,
                  to, tx, ty, so, sxy, sgo, sgxy,
-                 out_h, gin_h, gat_h, gwi_h, gwd_h, sm,
-                 out, gin, gat, gwi, gwd, part, rx_in, rx_mid, tot, res, cotp, hid, pre, act, gff, hlow, gpre, low, perm,
+                 out, gin, gat, gwi, gwd, sm,
+                 part, rx_in, rx_mid, tot, res, cotp, hid, pre, act, gff, hlow, gpre, low, perm,
                  q_s, k_s, v_s, prob, att, ob, obf, pairs, ob4, split_s, base, ga, gt, qt, dkt, dvt, dq, dk, dv, gacc,
                  ws, wo, wi, wd, outp, rows_s, vec_s, rx1, rx2, rx3, rx4, rxb, rxs,
                  s_in, s_mid, r_in, r_mid, cs, cr, cf, ss, sr, ls):
@@ -616,26 +616,29 @@
     lax.fori_loop(0, ROWS // BLOCK, back_step, 0)
     back(ROWS // BLOCK, ROWS % BLOCK)
 
+    gwd[...] = dot_tn(act[...], gff[...])
+    cube[1].step(0)
+    gwi[...] = dot_tn(hlow[...], gpre[...])
+    cube[0].step(0)
+    line.last([pieces - 2, pieces - 1])
+
     def late_step(m, carry):
+        attend_back(m, BLOCK)
+
+        @pl.when(m == 1)
+        def _():
+            cube[1].step(1)
+
         @pl.when(m == 2)
         def _():
-            line.last([pieces - 2, pieces - 1])
-            gwd[...] = dot_tn(act[...], gff[...])
-            cube[1].step(0)
-            gwi[...] = dot_tn(hlow[...], gpre[...])
-            cube[0].step(0)
-        attend_back(m, BLOCK)
+            cube[0].step(1)
         return carry
     lax.fori_loop(1, ROWS // BLOCK, late_step, 0)
     out[...] = outp[0:n, :]
-    store_out = [pltpu.make_async_copy(a, b, ls.at[i]) for i, (a, b) in enumerate(((out, out_h), (gwd, gwd_h), (gwi, gwi_h), (gat, gat_h), (gin, gin_h)))]
-    store_out[0].start()
     outp[...] = jnp.zeros_like(outp)
     attend_back(ROWS // BLOCK, ROWS % BLOCK)
     dk[...] = jnp.transpose(dkt[...]).astype(bf)
     dv[...] = jnp.transpose(dvt[...]).astype(bf)
-    cube[1].step(1)
-    cube[0].step(1)
 
     def produce(m, rows):
         r = block_rows(m, rows)
@@ -687,10 +690,13 @@
     def both_step(i):
         cube[1].step(i)
         cube[0].step(i)
-    jobs = {0: [(weight_grad, 0)], 1: [(weight_grad, 1)], 2: [(weight_grad, 2)], 3: [(cube[2].step, 0)], 4: [(both_step, 2), (bias_sums, 0)],
-            5: [(cube[2].step, 1), (table_sums, 0)], 6: [(table_sums, 1)], 7: [(table_sums, 2), (small_step, 0)],
-            8: [(both_step, 3)], 9: [(cube[2].step, 2), (small_step, 1)], 10: [(consume, 0)], 11: [(both_step, 4), (small_step, 2)],
-            12: [(cube[2].step, 3)], 13: [(small_step, 3)], 14: [(consume, 1), (cube[2].step, 4)], 17: [(both_step, 5)]}
+    jobs = {0: [(both_step, 2)], 1: [(cube[2].step, 1)], 2: [(bias_sums, 0), (table_sums, 0)], 3: [(table_sums, 1)],
+            4: [(table_sums, 2), (small_step, 0)], 6: [(both_step, 3), (small_step, 1)], 7: [(cube[2].step, 2)], 8: [(small_step, 2)],
+            9: [(consume, 0)], 10: [(small_step, 3)], 11: [(both_step, 4), (cube[2].step, 3)], 13: [(consume, 1)],
+            14: [(cube[2].step, 4)]}
+    for i in range(3):
+        weight_grad(i)
+    cube[2].step(0)
     ending = {p: [p - LAG] for p in range(LAG, pieces - 4)}
     ending.update({pieces - 4: [pieces - 8, pieces - 7], pieces - 3: [pieces - 6], pieces - 2: [pieces - 5, pieces - 4],
                    pieces - 1: [pieces - 3, pieces - 2]})
@@ -702,19 +708,14 @@
     for i in range(4, bits + 1):
         small_step(i)
     consume(2)
+    both_step(5)
     cube[2].step(5)
     consume(3)
+    consume(4)
     both_step(6)
-    store_out[1].start()
-    store_out[2].start()
     cube[2].step(6)
-    store_out[3].start()
-    consume(4)
     gin[...] = outp[0:n, :]
-    store_out[4].start()
     line.drain()
-    for c in store_out:
-        c.wait()
 
 
 def layer(bits, tok, cot, wq, wk, wv, wo, wi, wd, *small_args):
@@ -729,9 +730,8 @@
     more = max(bits - 3, 1)
     vm, hbm = pl.BlockSpec(memory_space=pltpu.VMEM), pl.BlockSpec(memory_space=pl.ANY)
     v_ = pltpu.VMEM
-    shapes = (sd((PAGE, d), f32), sd((PAGE, d), f32), sd((4 * width, d), f32), sd((d, f), f32), sd((f, d), f32), sd((24, d), f32))
-    scratch = [v_(s.shape, f32) for s in shapes[:5]]
-    scratch += [v_((R, d), f32)] * 7 + [v_((R, f), f32), v_((R, f), bf), v_((R, d), bf), v_((R, d), bf), v_((R, f), bf)]
+    shapes = (v_((PAGE, d), f32), v_((PAGE, d), f32), v_((4 * width, d), f32), v_((d, f), f32), v_((f, d), f32), v_((24, d), f32))
+    scratch = [v_((R, d), f32)] * 7 + [v_((R, f), f32), v_((R, f), bf), v_((R, d), bf), v_((R, d), bf), v_((R, f), bf)]
     scratch += [v_((W, d), bf), v_((W, W), bf)] + [v_((W, 256), bf)] * 3 + [v_((heads, R, W), f32)] + [v_((W, 256), bf)] * 3
     scratch += [v_((heads, 2, 128, 256), bf), v_((W, 512), bf), v_((W, d), bf), v_((heads, 128, 1280), f32)]
     scratch += [v_((BLOCK, 256), bf), v_((256, BLOCK), bf), v_((256, W), bf), v_((256, W), f32), v_((256, W), f32)]
@@ -742,24 +742,21 @@
     scratch += [pltpu.SemaphoreType.DMA((pieces,))] * 4 + [pltpu.SemaphoreType.DMA((3, 10 + 2 * more))] * 2
     scratch += [pltpu.SemaphoreType.REGULAR((3, 3))] + [pltpu.SemaphoreType.DMA((bits,))] * 2 + [pltpu.SemaphoreType.DMA((8,))]
     return pl.pallas_call(
-        functools.partial(layer_kernel, bits), out_shape=shapes, in_specs=[hbm] * 8 + [vm] * 19, out_specs=[hbm] * 5 + [vm],
+        functools.partial(layer_kernel, bits), out_shape=shapes, in_specs=[hbm] * 8 + [vm] * 19, out_specs=[vm] * 6,
         scratch_shapes=scratch,
-        compiler_params=pltpu.CompilerParams(collective_id=0, has_side_effects=True, vmem_limit_bytes=62 << 20),
+        compiler_params=pltpu.CompilerParams(collective_id=0, has_side_effects=True, vmem_limit_bytes=52 << 20),
         cost_estimate=pl.CostEstimate(flops=3 * 10 ** 10, bytes_accessed=20 << 20, transcendentals=heads * R * W),
     )(tok, cot, wq, wk, wv, wo, wi, wd, *small_args)
 
 
 def finish_kernel(out_in, gin_in, gat_in, gwi_in, gwd_in, sm, out, gin, gwq, gwk, gwv, gwo, gwi, gwd, *rest):
-    vectors, (b_out, b_gin, b_gat, b_gwi, b_gwd, sem_in, sem_out) = rest[:12], rest[12:]
+    vectors, sem = rest[:12], rest[12]
     width = gwo.shape[0]
     heads = vectors[9].shape[0]
-    whole = [(out_in, b_out, out), (gin_in, b_gin, gin), (gwi_in, b_gwi, gwi), (gwd_in, b_gwd, gwd)]
-    for i, g in enumerate((gwq, gwk, gwv, gwo)):
-        r = pl.ds(i * width, width)
-        whole.append((gat_in.at[r], b_gat.at[r], g))
-    inward = [pltpu.make_async_copy(a, b, sem_in.at[i]) for i, (a, b, _) in enumerate(whole)]
-    outward = [pltpu.make_async_copy(b, c, sem_out.at[i]) for i, (_, b, c) in enumerate(whole)]
-    for c in inward:
+    pairs = [(out_in, out), (gin_in, gin), (gwi_in, gwi), (gwd_in, gwd)]
+    pairs += [(gat_in.at[pl.ds(i * width, width)], g) for i, g in enumerate((gwq, gwk, gwv, gwo))]
+    copies = [pltpu.make_async_copy(a, b, sem.at[i]) for i, (a, b) in enumerate(pairs)]
+    for c in copies:
         c.start()
     for i in range(7):
         vectors[i][...] = sm[i, :]
@@ -768,11 +765,8 @@
     vectors[9][...] = sm[10:10 + heads, 0:BINS1]
     vectors[10][...] = sm[10 + heads:10 + 2 * heads, 0:BINS2]
     vectors[11][...] = sm[10 + 2 * heads:10 + 3 * heads, 0:BINS2]
-    for c, o in zip(inward, outward):
+    for c in copies:
         c.wait()
-        o.start()
-    for o in outward:
-        o.wait()
 
 
 def finish(heads, width, out, gin, gat, gwi, gwd, sm):
@@ -784,10 +778,10 @@
         + (sd((width,), f32),) * 2 + (sd((heads, BINS1), f32), sd((heads, BINS2), f32), sd((heads, BINS2), f32))
     vm, hbm = pl.BlockSpec(memory_space=pltpu.VMEM), pl.BlockSpec(memory_space=pl.ANY)
     return pl.pallas_call(
-        finish_kernel, out_shape=shapes, in_specs=[hbm] * 5 + [vm], out_specs=[hbm] * 8 + [vm] * 12,
-        scratch_shapes=[pltpu.VMEM(x.shape, f32) for x in (out, gin, gat, gwi, gwd)] + [pltpu.SemaphoreType.DMA((8,))] * 2,
-        compiler_params=pltpu.CompilerParams(vmem_limit_bytes=56 << 20),
-    )(out, gin, gat, gwi, gwd, sm)
+        finish_kernel, out_shape=shapes, in_specs=[vm] * 6, out_specs=[hbm] * 8 + [vm] * 12,
+        scratch_shapes=[pltpu.SemaphoreType.DMA((8,))],
+        compiler_params=pltpu.CompilerParams(vmem_limit_bytes=4 << 20),
+    )(*(pltpu.with_memory_space_constraint(x, pltpu.VMEM) for x in (out, gin, gat, gwi, gwd, sm)))
 
 
 def local(

time: 227 us -> 213 us (0.938); the launches traced: 227 us -> 211 us
  Pallas kernels: 226 us -> 210 us
    pallas_call x1, Pallas kernels: 217 us -> 205 us  [layer(): pl.pallas_call(functools.partial(layer_kernel, bits), out_shape=shapes, i...]
    pallas_call x1, Pallas kernels: 9.25 us -> 4.69 us  [finish(): pl.pallas_call(finish_kernel, out_shape=shapes, in_specs=[vm] * 6, out_sp...]
where the time goes in v5:
time: 213 us; the launch traced here: 211 us
  Pallas kernels  210 us (99%)
    pallas_call x1, Pallas kernels, layer(): pl.pallas_call(functools.partial(layer_kernel, bits), out_shape=shapes, i...  205 us
    pallas_call x1, Pallas kernels, finish(): pl.pallas_call(finish_kernel, out_shape=shapes, in_specs=[vm] * 6, out_sp...  4.69 us

profile of v5, /device:TPU:0, one launch (start us, length us, event | category | flops | bytes accessed | tf_op | source)
XLA Modules:
  0.0 210.8 jit_solution(13066870024205475402)
XLA Ops:
  0.7 205.2 %shard_map.410 = (f32[561,768]{1,0:T(8,128)S(1)}, f32[561,768]{1,0:T(8,128)S(1)}, f32[768,768]{1,0:T(8,128)S(1)}, f32[768,768]{1,0:T(8,128)S(1)}, f32[768,768]{1,0:T(8,128)S(1)}, /*index=5*/f32[24,768]{1,0:T(8,128)S(1)}) custom-call(f32[561,768]{1,0:T(8,128)} %tok_h.1, f32[561,768]{1,0:T(8,128)} %cot_h.1, f32[192,768]{1,0:T(8,128)} %bitcast.6, ...), custom_call_target="tpu_custom_call" | custom-call | flops 30000001024 | bytes 20971520 | tf_op jit(solution)/shard_map/pallas_call | solution.py:744
  205.9 4.7 %shard_map.411 = (f32[561,768]{1,0:T(8,128)}, f32[561,768]{1,0:T(8,128)}, f32[192,768]{1,0:T(8,128)}, f32[192,768]{1,0:T(8,128)}, f32[192,768]{1,0:T(8,128)}, /*...) custom-call(f32[561,768]{1,0:T(8,128)S(1)} %get-tuple-element.46.out, ...), custom_call_target="tpu_custom_call" | custom-call | tf_op jit(solution)/shard_map/pallas_call | solution.py:780
